TPU v7x, 32 devices: a whole 2x2x4 slice. The times are simulated.
32 devices in a mesh: dp: 8 (over z, x), tensor: 4 (over y, core).
Axes of the slice: x: 2, y: 2, z: 4, core: 2. Of those that a mesh axis runs over, the one named last changes fastest.
Arguments:
- hidden_in: float32 [8, 1024, 1280], P('dp', 'tensor'), may hold values from -0.2 to 0.2
- lengths: int32 [8], P('dp'), may hold values from 256 to 1024
- teacher: float32 [8, 1024, 1280], P('dp', 'tensor'), may hold values from -0.2 to 0.2
- w_query: bfloat16 [1280, 1280], P('dp', 'tensor'), may hold values from -0.15625 to 0.15625
- w_key: bfloat16 [1280, 1280], P('dp', 'tensor'), may hold values from -0.15625 to 0.15625
- w_value: bfloat16 [1280, 1280], P('dp', 'tensor'), may hold values from -0.15625 to 0.15625
- w_attn_out: bfloat16 [1280, 1280], P('tensor', 'dp'), may hold values from -0.15625 to 0.15625
- w_up: bfloat16 [1280, 5120], P('dp', 'tensor'), may hold values from -0.15625 to 0.15625
- w_gate: bfloat16 [1280, 5120], P('dp', 'tensor'), may hold values from -0.15625 to 0.15625
- w_down: bfloat16 [5120, 1280], P('tensor', 'dp'), may hold values from -0.078125 to 0.078125
- s_qk: float32 [1280], replicated, may hold values from 0.8 to 1.6
- alpha_attn: float32 [1280], replicated, may hold values from 0.15 to 0.6
- alpha_mlp: float32 [1280], replicated, may hold values from 0.15 to 0.6
- s_up: float32 [5120], replicated, may hold values from 0.5 to 2
- s_gate: float32 [5120], replicated, may hold values from 0.5 to 2
Outputs:
- loss: float32 [], replicated
- output: float32 [8, 1024, 1280], P('dp', 'tensor')
- grad_input: float32 [8, 1024, 1280], P('dp', 'tensor')
- grad_w_query: float32 [1280, 1280], P('dp', 'tensor')
- grad_w_key: float32 [1280, 1280], P('dp', 'tensor')
- grad_w_value: float32 [1280, 1280], P('dp', 'tensor')
- grad_w_attn_out: float32 [1280, 1280], P('tensor', 'dp')
- grad_w_up: float32 [1280, 5120], P('dp', 'tensor')
- grad_w_gate: float32 [1280, 5120], P('dp', 'tensor')
- grad_w_down: float32 [5120, 1280], P('tensor', 'dp')
- grad_s_qk: float32 [1280], replicated
- grad_alpha_attn: float32 [1280], replicated
- grad_alpha_mlp: float32 [1280], replicated
- grad_s_up: float32 [5120], replicated
- grad_s_gate: float32 [5120], replicated
All inputs are finite; a program needn't handle non-finite values.
Results may differ from a plain program's by a relative error of at most 0.018.
Values may be sent and summed in bfloat16 or wider, within the bound.
No kernel may reach another device: no remote copies, remote signals or barrier semaphores. Data moves between devices by JAX's collectives and lax.ppermute only.
A program may use at most 192 MiB of HBM per device.

v0:
```python
import math

import jax
import jax.numpy as jnp
from jax import lax
from jax.sharding import PartitionSpec as P

HEAD = 64


EPSILON = 1e-06


def normalize(vector):
    factor = lax.rsqrt(jnp.sum(vector * vector, axis=-1, keepdims=True) + EPSILON)
    return (vector * factor, factor)


def norm_back(cotangent, normed, factor):
    return factor * (cotangent - normed * jnp.sum(cotangent * normed, axis=-1, keepdims=True))


def gather_stream(values):
    return lax.all_gather(values, "tensor", axis=1, tiled=True)


def scatter_branch(partial_sum):
    return lax.psum_scatter(partial_sum, "tensor", scatter_dimension=1, tiled=True)


def gather_branch_grad(values):
    return lax.all_gather(values, "tensor", axis=1, tiled=True)


def scatter_stream_grad(partial_sum):
    return lax.psum_scatter(
        partial_sum.astype(jnp.bfloat16), "tensor", scatter_dimension=1, tiled=True
    ).astype(jnp.float32)


def masked_scores(query_block, k_seq, first_row, length):
    slot_count = k_seq.shape[0]
    block_rows = query_block.shape[0]
    scores = math.sqrt(query_block.shape[2]) * jnp.einsum(
        "qhd,khd->hqk", query_block, k_seq, preferred_element_type=jnp.float32
    )
    key_ids = lax.broadcasted_iota(jnp.int32, (1, slot_count), 1)
    query_ids = first_row + lax.broadcasted_iota(jnp.int32, (block_rows, 1), 0)
    allowed = (key_ids <= query_ids) & (key_ids < length)
    return jnp.where(allowed[None], scores, -1e30)


def attend(q_seq, k_seq, v_seq, length, block_rows):
    slot_count = q_seq.shape[0]

    def one_block(first_row):
        query_block = lax.dynamic_slice_in_dim(q_seq, first_row, block_rows, 0)
        scores = masked_scores(query_block, k_seq, first_row, length)
        row_max = jnp.max(scores, axis=-1, keepdims=True)
        exponent = jnp.exp(scores - row_max)
        row_total = jnp.sum(exponent, axis=-1, keepdims=True)
        probabilities = (exponent / row_total).astype(jnp.bfloat16)
        block_out = jnp.einsum(
            "hqk,khd->qhd", probabilities, v_seq, preferred_element_type=jnp.float32
        )
        return (block_out, (row_max + jnp.log(row_total))[..., 0])

    starts = jnp.arange(slot_count // block_rows, dtype=jnp.int32) * block_rows
    block_outs, log_totals = lax.map(one_block, starts)
    return (block_outs.reshape(q_seq.shape), log_totals)


def attend_back(q_seq, k_seq, v_seq, log_totals, grad_seq, length, block_rows):
    slot_count = q_seq.shape[0]
    root_scale = math.sqrt(q_seq.shape[2])

    def one_block(running, block_item):
        first_row, block_totals = block_item
        grad_keys, grad_values = running
        query_block = lax.dynamic_slice_in_dim(q_seq, first_row, block_rows, 0)
        grad_block = lax.dynamic_slice_in_dim(grad_seq, first_row, block_rows, 0)
        scores = masked_scores(query_block, k_seq, first_row, length)
        probabilities = jnp.exp(scores - block_totals[..., None])
        grad_probs = jnp.einsum(
            "qhd,khd->hqk", grad_block, v_seq, preferred_element_type=jnp.float32
        )
        row_delta = jnp.sum(grad_probs * probabilities, axis=-1, keepdims=True)
        grad_scores = (probabilities * (grad_probs - row_delta)).astype(jnp.bfloat16)
        grad_query = root_scale * jnp.einsum(
            "hqk,khd->qhd", grad_scores, k_seq, preferred_element_type=jnp.float32
        )
        grad_keys = grad_keys + root_scale * jnp.einsum(
            "hqk,qhd->khd", grad_scores, query_block, preferred_element_type=jnp.float32
        )
        grad_values = grad_values + jnp.einsum(
            "hqk,qhd->khd",
            probabilities.astype(jnp.bfloat16),
            grad_block,
            preferred_element_type=jnp.float32,
        )
        return ((grad_keys, grad_values), grad_query)

    starts = jnp.arange(slot_count // block_rows, dtype=jnp.int32) * block_rows
    zeros_kv = jnp.zeros(q_seq.shape, jnp.float32)
    (grad_keys, grad_values), grad_queries = lax.scan(
        one_block, (zeros_kv, zeros_kv), (starts, log_totals)
    )
    return (grad_queries.reshape(q_seq.shape), grad_keys, grad_values)


def on_device(
    hidden_in,
    lengths,
    teacher,
    w_query,
    w_key,
    w_value,
    w_attn_out,
    w_up,
    w_gate,
    w_down,
    s_qk,
    alpha_attn,
    alpha_mlp,
    s_up,
    s_gate,
):
    tensor_size = lax.axis_size("tensor")
    dp_size = lax.axis_size("dp")
    tensor_rank = lax.axis_index("tensor")
    seq_count, local_slots, model_width = hidden_in.shape
    slot_count = local_slots * tensor_size
    row_count = seq_count * slot_count
    heads_width = w_query.shape[1]
    head_count = heads_width // HEAD
    ff_local = w_up.shape[1]
    block_rows = min(512, slot_count)
    gate_root = math.sqrt(model_width)
    token_count = lax.psum(jnp.sum(lengths.astype(jnp.float32)), "dp")
    query_full, key_full, value_full, attn_out_full = (
        lax.all_gather(w_query, "dp", axis=0, tiled=True),
        lax.all_gather(w_key, "dp", axis=0, tiled=True),
        lax.all_gather(w_value, "dp", axis=0, tiled=True),
        lax.all_gather(w_attn_out, "dp", axis=1, tiled=True),
    )
    w_project = jnp.concatenate([query_full, key_full, value_full], axis=1)
    stream_low = hidden_in.astype(jnp.bfloat16)
    gathered = gather_stream(stream_low).reshape(row_count, model_width)
    projected = jnp.dot(gathered, w_project, preferred_element_type=jnp.float32)
    q_raw = projected[:, :heads_width].reshape(row_count, head_count, HEAD)
    k_raw = projected[:, heads_width : 2 * heads_width].reshape(row_count, head_count, HEAD)
    v_low = (
        projected[:, 2 * heads_width :]
        .astype(jnp.bfloat16)
        .reshape(seq_count, slot_count, head_count, HEAD)
    )
    q_unit, q_factor = normalize(q_raw)
    k_unit, k_factor = normalize(k_raw)
    qk_gain = lax.dynamic_slice_in_dim(s_qk, tensor_rank * heads_width, heads_width).reshape(
        head_count, HEAD
    )
    q_low = (q_unit * qk_gain).astype(jnp.bfloat16).reshape(seq_count, slot_count, head_count, HEAD)
    k_low = (k_unit * qk_gain).astype(jnp.bfloat16).reshape(seq_count, slot_count, head_count, HEAD)

    def forward_seq(seq_item):
        return attend(seq_item[0], seq_item[1], seq_item[2], seq_item[3], block_rows)

    attended, log_totals = lax.map(forward_seq, (q_low, k_low, v_low, lengths))
    attended_low = attended.reshape(row_count, heads_width).astype(jnp.bfloat16)
    attn_part = jnp.dot(attended_low, attn_out_full, preferred_element_type=jnp.float32)
    attn_sum = scatter_branch(attn_part.reshape(seq_count, slot_count, model_width))
    attn_unit, attn_factor = normalize(attn_sum)
    first_out, first_factor = normalize(hidden_in + alpha_attn * (attn_unit - hidden_in))
    up_full, gate_full, down_full = (
        lax.all_gather(w_up, "dp", axis=0, tiled=True),
        lax.all_gather(w_gate, "dp", axis=0, tiled=True),
        lax.all_gather(w_down, "dp", axis=1, tiled=True),
    )
    w_pair = jnp.concatenate([up_full, gate_full], axis=1)
    mlp_in = gather_stream(first_out.astype(jnp.bfloat16)).reshape(row_count, model_width)
    up_gate = jnp.dot(mlp_in, w_pair, preferred_element_type=jnp.float32)
    up_raw = up_gate[:, :ff_local]
    gate_raw = up_gate[:, ff_local:]
    up_gain = lax.dynamic_slice_in_dim(s_up, tensor_rank * ff_local, ff_local)
    gate_gain = lax.dynamic_slice_in_dim(s_gate, tensor_rank * ff_local, ff_local) * gate_root
    scaled_up = up_raw * up_gain
    scaled_gate = gate_raw * gate_gain
    sigmoid_gate = jax.nn.sigmoid(scaled_gate)
    activated = scaled_gate * sigmoid_gate
    hidden_low = (scaled_up * activated).astype(jnp.bfloat16)
    mlp_part = jnp.dot(hidden_low, down_full, preferred_element_type=jnp.float32)
    mlp_sum = scatter_branch(mlp_part.reshape(seq_count, slot_count, model_width))
    mlp_unit, mlp_factor = normalize(mlp_sum)
    output, out_factor = normalize(first_out + alpha_mlp * (mlp_unit - first_out))
    slot_ids = tensor_rank * local_slots + lax.broadcasted_iota(
        jnp.int32, (seq_count, local_slots), 1
    )
    valid_mask = (slot_ids < lengths[:, None]).astype(jnp.float32)
    difference = output - teacher
    error_sum = jnp.sum(jnp.sum(difference * difference, axis=-1) * valid_mask)
    total_slots = row_count * dp_size
    grad_output = 2.0 * total_slots / token_count * difference * valid_mask[..., None]
    grad_mixed_two = norm_back(grad_output, output, out_factor)
    grad_alpha_mlp = jnp.sum(grad_mixed_two * (mlp_unit - first_out), axis=(0, 1))
    grad_first = grad_mixed_two * (1.0 - alpha_mlp)
    grad_mlp_sum = norm_back(grad_mixed_two * alpha_mlp, mlp_unit, mlp_factor).astype(jnp.bfloat16)
    grad_mlp_rows = gather_branch_grad(grad_mlp_sum).reshape(row_count, model_width)
    up_back, gate_back, down_back = (
        lax.all_gather(w_up, "dp", axis=0, tiled=True),
        lax.all_gather(w_gate, "dp", axis=0, tiled=True),
        lax.all_gather(w_down, "dp", axis=1, tiled=True),
    )
    pair_back = jnp.concatenate([up_back, gate_back], axis=1)
    grad_down = jnp.einsum(
        "rf,rd->fd", hidden_low, grad_mlp_rows, preferred_element_type=jnp.float32
    )
    grad_hidden = jnp.einsum(
        "rd,fd->rf", grad_mlp_rows, down_back, preferred_element_type=jnp.float32
    )
    grad_scaled_up = grad_hidden * activated
    grad_scaled_gate = (
        grad_hidden * scaled_up * sigmoid_gate * (1.0 + scaled_gate * (1.0 - sigmoid_gate))
    )
    grad_up_gain = jnp.sum(grad_scaled_up * up_raw, axis=0)
    grad_gate_gain = jnp.sum(grad_scaled_gate * gate_raw, axis=0) * gate_root
    grad_pair = jnp.concatenate(
        [grad_scaled_up * up_gain, grad_scaled_gate * gate_gain], axis=1
    ).astype(jnp.bfloat16)
    grad_w_pair = jnp.einsum("rd,rf->df", mlp_in, grad_pair, preferred_element_type=jnp.float32)
    grad_mlp_in = jnp.einsum("rf,df->rd", grad_pair, pair_back, preferred_element_type=jnp.float32)
    grad_first = grad_first + scatter_stream_grad(
        grad_mlp_in.reshape(seq_count, slot_count, model_width)
    )
    grad_w_up, grad_w_gate, grad_w_down = (
        lax.psum_scatter(grad_w_pair[:, :ff_local], "dp", scatter_dimension=0, tiled=True),
        lax.psum_scatter(grad_w_pair[:, ff_local:], "dp", scatter_dimension=0, tiled=True),
        lax.psum_scatter(grad_down, "dp", scatter_dimension=1, tiled=True),
    )
    grad_mixed = norm_back(grad_first, first_out, first_factor)
    grad_alpha_attn = jnp.sum(grad_mixed * (attn_unit - hidden_in), axis=(0, 1))
    grad_input = grad_mixed * (1.0 - alpha_attn)
    grad_attn_sum = norm_back(grad_mixed * alpha_attn, attn_unit, attn_factor).astype(jnp.bfloat16)
    grad_attn_rows = gather_branch_grad(grad_attn_sum).reshape(row_count, model_width)
    query_back, key_back, value_back, attn_out_back = (
        lax.all_gather(w_query, "dp", axis=0, tiled=True),
        lax.all_gather(w_key, "dp", axis=0, tiled=True),
        lax.all_gather(w_value, "dp", axis=0, tiled=True),
        lax.all_gather(w_attn_out, "dp", axis=1, tiled=True),
    )
    project_back = jnp.concatenate([query_back, key_back, value_back], axis=1)
    grad_attn_out = jnp.einsum(
        "rc,rd->cd", attended_low, grad_attn_rows, preferred_element_type=jnp.float32
    )
    grad_attended = jnp.einsum(
        "rd,cd->rc", grad_attn_rows, attn_out_back, preferred_element_type=jnp.float32
    )
    grad_attended = grad_attended.astype(jnp.bfloat16).reshape(
        seq_count, slot_count, head_count, HEAD
    )

    def backward_seq(seq_item):
        return attend_back(
            seq_item[0], seq_item[1], seq_item[2], seq_item[3], seq_item[4], seq_item[5], block_rows
        )

    grad_q_low, grad_k_low, grad_v_low = lax.map(
        backward_seq, (q_low, k_low, v_low, log_totals, grad_attended, lengths)
    )
    grad_q_low = grad_q_low.reshape(row_count, head_count, HEAD)
    grad_k_low = grad_k_low.reshape(row_count, head_count, HEAD)
    grad_gain = jnp.sum(grad_q_low * q_unit + grad_k_low * k_unit, axis=0).reshape(heads_width)
    grad_q = norm_back(grad_q_low * qk_gain, q_unit, q_factor).reshape(row_count, heads_width)
    grad_k = norm_back(grad_k_low * qk_gain, k_unit, k_factor).reshape(row_count, heads_width)
    grad_project = jnp.concatenate(
        [grad_q, grad_k, grad_v_low.reshape(row_count, heads_width)], axis=1
    ).astype(jnp.bfloat16)
    grad_w_project = jnp.einsum(
        "rd,rc->dc", gathered, grad_project, preferred_element_type=jnp.float32
    )
    grad_gathered = jnp.einsum(
        "rc,dc->rd", grad_project, project_back, preferred_element_type=jnp.float32
    )
    grad_input = grad_input + scatter_stream_grad(
        grad_gathered.reshape(seq_count, slot_count, model_width)
    )
    grad_w_query, grad_w_key, grad_w_value, grad_w_attn_out = (
        lax.psum_scatter(grad_w_project[:, :heads_width], "dp", scatter_dimension=0, tiled=True),
        lax.psum_scatter(
            grad_w_project[:, heads_width : 2 * heads_width], "dp", scatter_dimension=0, tiled=True
        ),
        lax.psum_scatter(
            grad_w_project[:, 2 * heads_width :], "dp", scatter_dimension=0, tiled=True
        ),
        lax.psum_scatter(grad_attn_out, "dp", scatter_dimension=1, tiled=True),
    )
    full_gain = lax.dynamic_update_slice_in_dim(
        jnp.zeros((model_width,), jnp.float32), grad_gain, tensor_rank * heads_width, 0
    )
    full_up = lax.dynamic_update_slice_in_dim(
        jnp.zeros((ff_local * tensor_size,), jnp.float32), grad_up_gain, tensor_rank * ff_local, 0
    )
    full_gate = lax.dynamic_update_slice_in_dim(
        jnp.zeros((ff_local * tensor_size,), jnp.float32), grad_gate_gain, tensor_rank * ff_local, 0
    )
    reduced = lax.psum(
        (error_sum, grad_alpha_attn, grad_alpha_mlp, full_gain, full_up, full_gate),
        ("dp", "tensor"),
    )
    loss = reduced[0] / token_count
    return (
        loss,
        output,
        grad_input,
        grad_w_query,
        grad_w_key,
        grad_w_value,
        grad_w_attn_out,
        grad_w_up,
        grad_w_gate,
        grad_w_down,
        reduced[3],
        reduced[1],
        reduced[2],
        reduced[4],
        reduced[5],
    )


def solution(mesh):
    in_specs = (
        P("dp", "tensor", None),
        P("dp"),
        P("dp", "tensor", None),
        P("dp", "tensor"),
        P("dp", "tensor"),
        P("dp", "tensor"),
        P("tensor", "dp"),
        P("dp", "tensor"),
        P("dp", "tensor"),
        P("tensor", "dp"),
        P(),
        P(),
        P(),
        P(),
        P(),
    )
    out_specs = (
        P(),
        P("dp", "tensor", None),
        P("dp", "tensor", None),
        P("dp", "tensor"),
        P("dp", "tensor"),
        P("dp", "tensor"),
        P("tensor", "dp"),
        P("dp", "tensor"),
        P("dp", "tensor"),
        P("tensor", "dp"),
        P(),
        P(),
        P(),
        P(),
        P(),
    )
    return jax.shard_map(
        on_device, mesh=mesh, in_specs=in_specs, out_specs=out_specs, check_vma=False
    )
```

profile of v0, /device:TPU:0, one launch (start us, length us, event | category | flops | bytes accessed | tf_op | source)
XLA Modules:
  0.0 1355.3 jit_solution(4331772379990999723)
XLA Ops:
  11.4 34.4 %all_gather.40 = bf16[1280,320]{1,0:T(8,128)(2,1)S(1)} all-gather(bf16[160,320]{1,0:T(8,128)(2,1)S(1)} %copy-done.36), channel_id=1, replica_groups=mesh['dp'=8,'tensor'=4] {'dp'}, dimensions={0}, use_global_device_ids=true | all-gather | bytes 921600 | tf_op jit(solution)/shard_map/all_gather | solution.py:141
  45.8 33.3 %all_gather.41 = bf16[1280,320]{1,0:T(8,128)(2,1)S(1)} all-gather(bf16[160,320]{1,0:T(8,128)(2,1)S(1)} %copy-done.37), channel_id=1, replica_groups=mesh['dp'=8,'tensor'=4] {'dp'}, dimensions={0}, use_global_device_ids=true | all-gather | bytes 921600 | tf_op jit(solution)/shard_map/all_gather | solution.py:142
  79.1 34.5 %all_gather.42 = bf16[1280,320]{1,0:T(8,128)(2,1)} all-gather(bf16[160,320]{1,0:T(8,128)(2,1)S(1)} %copy-done.38), channel_id=1, replica_groups=mesh['dp'=8,'tensor'=4] {'dp'}, dimensions={0}, use_global_device_ids=true | all-gather | bytes 921600 | tf_op jit(solution)/shard_map/all_gather | solution.py:143
  113.6 35.0 %all_gather.44 = bf16[320,1280]{0,1:T(8,128)(2,1)} all-gather(bf16[320,160]{0,1:T(8,128)(2,1)S(1)} %copy-done.39), channel_id=1, replica_groups=mesh['dp'=8,'tensor'=4] {'dp'}, dimensions={1}, use_global_device_ids=true | all-gather | bytes 921600 | tf_op jit(solution)/shard_map/all_gather | solution.py:144
  148.6 5.5 fusion.57
  157.5 27.0 %while.49 = (s32[]{:T(128)}, bf16[2,512,5,64]{1,3,2,0:T(8,128)(2,1)S(1)}, f32[2,5,512]{2,1,0:T(8,128)S(1)}, s32[2]{0:T(128)S(1)}, s32[]{:T(128)}, /*index=5*/bf1...) while((s32[]{:T(128)}, ...), condition=%wide.region_5.6_spmd.clone, body=%wide.region_2.5_spmd.sunk.clone | while | flops 703593472 | bytes 35967132 | solution.py:69
  167.1 3.8 fusion.148
  180.6 3.8 fusion.148
  186.1 3.9 convolution_bitcast_fusion.1
  191.5 51.1 %reduce-scatter.18.cloned.1.call-done = f32[1,256,1280]{2,1,0:T(8,128)} async-done(((f32[1,1024,1280]{2,1,0:T(8,128)}), f32[1,256,1280]{2,1,0:T(8,128)}) %reduce-scatter.18.cloned.1.call-update) | async-done | bytes 1310736 | tf_op jit(solution)/shard_map/reduce_scatter | solution.py:28
  249.6 5.7 all-gather.12.cloned.1.call-done
  255.3 3.9 constant_dynamic-update-slice_fusion.1
  259.3 58.6 %all-gather.14.cloned.1.call-done = bf16[1280,1280]{1,0:T(8,128)(2,1)} async-done(((bf16[160,1280]{1,0:T(8,128)(2,1)}), bf16[1280,1280]{1,0:T(8,128)(2,1)}) %all-gather.14.cloned.1.call-update) | async-done | bytes 3276816 | tf_op jit(solution)/shard_map/all_gather | solution.py:176
  317.8 3.9 constant_dynamic-update-slice_fusion
  321.7 22.3 %all-gather.10.cloned.1.call-done = bf16[1,1024,1280]{2,1,0:T(8,128)(2,1)} async-done(((bf16[1,256,1280]{2,1,0:T(8,128)(2,1)}), bf16[1,1024,1280]{2,1,0:T(8,128)(2,1)}) %all-gather.10.cloned.1.call-update) | async-done | bytes 2621456 | tf_op jit(solution)/shard_map/all_gather | solution.py:24
  344.0 9.9 fusion.52
  353.9 4.0 copy-done.12
  360.6 47.4 %all-gather.16.cloned.1.call-done = bf16[1280,1280]{0,1:T(8,128)(2,1)} async-done(((bf16[1280,160]{0,1:T(8,128)(2,1)}), bf16[1280,1280]{0,1:T(8,128)(2,1)}) %all-gather.16.cloned.1.call-update) | async-done | bytes 3276816 | tf_op jit(solution)/shard_map/all_gather | solution.py:177
  408.0 8.6 convolution_bitcast_fusion
  417.3 20.3 %psum.50 = f32[]{:T(128)} all-reduce(f32[]{:T(128)} %bitcast.13), channel_id=1, replica_groups=mesh['dp'=8,'tensor'=4] {'dp'}, use_global_device_ids=true, to_apply=%region_15.16 | all-reduce | flops 1 | bytes 8 | tf_op jit(solution)/shard_map/psum | solution.py:139
  438.4 28.5 %reduce-scatter.20.cloned.1.call-done = f32[1,256,1280]{2,1,0:T(8,128)} async-done(((f32[1,1024,1280]{2,1,0:T(8,128)}), f32[1,256,1280]{2,1,0:T(8,128)}) %reduce-scatter.20.cloned.1.call-update) | async-done | bytes 1310736 | tf_op jit(solution)/shard_map/reduce_scatter | solution.py:28
  475.9 25.1 %all-gather.18.cloned.1.call-done = bf16[1,1024,1280]{2,1,0:T(8,128)(2,1)} async-done(((bf16[1,256,1280]{2,1,0:T(8,128)(2,1)}), bf16[1,1024,1280]{2,1,0:T(8,128)(2,1)}) %all-gather.18.cloned.1.call-update) | async-done | bytes 2621456 | tf_op jit(solution)/shard_map/all_gather | solution.py:32
  500.9 11.6 multiply_reduce_fusion.1
  514.8 11.1 fusion.41
  526.0 34.7 %reduce-scatter.22.cloned.1.call-done = bf16[1,256,1280]{2,1,0:T(8,128)(2,1)} async-done(((bf16[1,1024,1280]{2,1,0:T(8,128)(2,1)}), bf16[1,256,1280]{2,1,0:T(8,128)(2,1)}) %reduce-scatter.22.cloned.1.call-update) | async-done | bytes 655376 | tf_op jit(solution)/shard_map/reduce_scatter | solution.py:36
  568.3 3.2 reshape.359
  571.5 22.3 %all-gather.20.cloned.1.call-done = bf16[1,1024,1280]{2,1,0:T(8,128)(2,1)} async-done(((bf16[1,256,1280]{2,1,0:T(8,128)(2,1)}), bf16[1,1024,1280]{2,1,0:T(8,128)(2,1)}) %all-gather.20.cloned.1.call-update) | async-done | bytes 2621456 | tf_op jit(solution)/shard_map/all_gather | solution.py:32
  593.8 3.9 fusion.64
  597.7 44.4 %while.50 = (s32[]{:T(128)}, f32[1024,5,64]{0,2,1:T(8,128)S(1)}, f32[1024,5,64]{0,2,1:T(8,128)}, f32[2,512,5,64]{1,3,2,0:T(8,128)}, s32[2]{0:T(128)S(1)}, /*inde...) while((s32[]{:T(128)}, f32[1024,5,64]{0,2,1:T(8,128)S(1)}, ...), condition=%wide.region_23.24_spmd.clone.clone, body=%wide.region_21.23_spmd.clone.sunk.clone | while | flops 1719892992 | bytes 103113000 | solution.py:105
  603.8 4.1 fusion.161
  607.9 4.0 multiply_reduce_fusion.19
  612.0 3.1 multiply_convert_fusion.11
  625.1 5.5 fusion.161
  630.6 4.1 multiply_reduce_fusion.19
  650.5 5.1 fusion.42
  656.7 4.6 fusion.43
  661.4 5.1 convolution_bitcast_fusion.2
  676.4 8.8 fusion.47
  685.3 13.0 fusion.40
  698.3 10.5 fusion.83
  713.1 41.4 %all-reduce = (f32[]{:T(128)}, f32[1280]{0:T(1024)}, f32[1280]{0:T(1024)}, f32[1280]{0:T(1024)}, f32[5120]{0:T(1024)}, /*index=5*/f32[5120]{0:T(1024)}) all-reduce(f32[]{:T(128)} %select_reduce_fusion, f32[1280]{0:T(1024)S(1)} %dynamic_update_slice.32, f32[1280]{0:T(1024)S(1)} %copy-done.43, ...), channel_id=1, replica_groups=mesh['dp'=8,'tensor'=4] {'dp','tensor'}, use_global_device_ids=true, to_apply=%region_14.15 | all-reduce | flops 14081 | bytes 112648 | tf_op jit(solution)/shard_map/psum | solution.py:305
  758.6 3.2 reduce-scatter.26.cloned.1.call-done
  761.8 70.0 %reduce-scatter.38.cloned.1.call-done = f32[160,320]{1,0:T(8,128)} async-done(((f32[1280,320]{1,0:T(8,128)}), f32[160,320]{1,0:T(8,128)}) %reduce-scatter.38.cloned.1.call-update) | async-done | bytes 204816
  831.9 70.0 %reduce-scatter.36.cloned.1.call-done = f32[160,320]{1,0:T(8,128)} async-done(((f32[1280,320]{1,0:T(8,128)}), f32[160,320]{1,0:T(8,128)}) %reduce-scatter.36.cloned.1.call-update) | async-done | bytes 204816
  901.8 70.1 %reduce-scatter.34.cloned.1.call-done = f32[160,320]{1,0:T(8,128)} async-done(((f32[1280,320]{1,0:T(8,128)}), f32[160,320]{1,0:T(8,128)}) %reduce-scatter.34.cloned.1.call-update) | async-done | bytes 204816
  971.9 124.7 %reduce-scatter.32.cloned.1.call-done = f32[1280,160]{0,1:T(8,128)} async-done(((f32[1280,1280]{0,1:T(8,128)}), f32[1280,160]{0,1:T(8,128)}) %reduce-scatter.32.cloned.1.call-update) | async-done | bytes 819216 | tf_op jit(solution)/shard_map/reduce_scatter | solution.py:237
  1096.6 125.0 %reduce-scatter.30.cloned.1.call-done = f32[160,1280]{1,0:T(8,128)} async-done(((f32[1280,1280]{1,0:T(8,128)}), f32[160,1280]{1,0:T(8,128)}) %reduce-scatter.30.cloned.1.call-update) | async-done | bytes 819216 | tf_op jit(solution)/shard_map/reduce_scatter | solution.py:236
  1221.6 124.7 %reduce-scatter.28.cloned.1.call-done = f32[160,1280]{1,0:T(8,128)} async-done(((f32[1280,1280]{1,0:T(8,128)}), f32[160,1280]{1,0:T(8,128)}) %reduce-scatter.28.cloned.1.call-update) | async-done | bytes 819216 | tf_op jit(solution)/shard_map/reduce_scatter | solution.py:235
  (236 shorter events, 99.2 us)
Async XLA Ops:
  8.0 3.4 copy-start.36
  8.0 37.8 %copy-start.37 = (bf16[160,320]{1,0:T(8,128)(2,1)S(1)}, bf16[160,320]{1,0:T(8,128)(2,1)}, u32[]{:S(2)}) copy-start(bf16[160,320]{1,0:T(8,128)(2,1)} %param.23) | copy-start | bytes 307204
  8.0 71.0 %copy-start.38 = (bf16[160,320]{1,0:T(8,128)(2,1)S(1)}, bf16[160,320]{1,0:T(8,128)(2,1)}, u32[]{:S(2)}) copy-start(bf16[160,320]{1,0:T(8,128)(2,1)} %param.24) | copy-start | bytes 307204
  8.0 140.5 %all-gather.8.cloned.1.call-start = ((), (), s32[]{:S(2)}) async-start(), calls=%async_computation.11 | async-start | bytes 3276800 | tf_op jit(solution)/shard_map/all_gather | solution.py:24
  10.4 103.2 %copy-start.39 = (bf16[320,160]{0,1:T(8,128)(2,1)S(1)}, bf16[320,160]{0,1:T(8,128)(2,1)}, u32[]{:S(2)}) copy-start(bf16[320,160]{0,1:T(8,128)(2,1)} %param.25) | copy-start | bytes 307204
  10.4 232.1 %reduce-scatter.18.cloned.1.call-start = ((), (), s32[]{:S(2)}) async-start(), calls=%async_computation.12 | async-start | bytes 6553600 | tf_op jit(solution)/shard_map/reduce_scatter | solution.py:28
  11.3 142.8 %copy-start.44 = (f32[320]{0:T(512)}, f32[320]{0:T(512)S(1)}, u32[]{:S(2)}) copy-start(f32[320]{0:T(512)S(1)} %dynamic_slice.52) | copy-start | bytes 3844
  11.4 145.0 %copy-start.40 = (f32[5,64]{1,0:T(8,128)}, f32[5,64]{1,0:T(8,128)S(1)}, u32[]{:S(2)}) copy-start(f32[5,64]{1,0:T(8,128)S(1)} %mul.410) | copy-start | bytes 3844
  45.8 102.8 %copy-start.20 = (bf16[1280,320]{1,0:T(8,128)(2,1)}, bf16[1280,320]{1,0:T(8,128)(2,1)S(1)}, u32[]{:S(2)}) copy-start(bf16[1280,320]{1,0:T(8,128)(2,1)S(1)} %all_gather.40) | copy-start | bytes 2457604
  79.1 75.0 %copy-start.22 = (bf16[1280,320]{1,0:T(8,128)(2,1)}, bf16[1280,320]{1,0:T(8,128)(2,1)S(1)}, u32[]{:S(2)}) copy-start(bf16[1280,320]{1,0:T(8,128)(2,1)S(1)} %all_gather.41) | copy-start | bytes 2457604
  154.1 1.9 copy-start.13
  184.5 1.6 copy-start.25
  190.0 54.0 %copy-start.34 = (f32[1280]{0:T(1024)S(1)}, f32[1280]{0:T(1024)}, u32[]{:S(2)}) copy-start(f32[1280]{0:T(1024)} %param.30) | copy-start | bytes 15364
  190.0 65.3 %all-gather.12.cloned.1.call-start = ((), (), s32[]{:S(2)}) async-start(), calls=%async_computation.14 | async-start | bytes 3686400 | tf_op jit(solution)/shard_map/all_gather | solution.py:175
  190.6 127.2 %all-gather.14.cloned.1.call-start = ((), (), s32[]{:S(2)}) async-start(), calls=%async_computation.15 | async-start | bytes 3686400 | tf_op jit(solution)/shard_map/all_gather | solution.py:176
  191.2 152.9 %all-gather.10.cloned.1.call-start = ((), (), s32[]{:S(2)}) async-start(), calls=%async_computation.13 | async-start | bytes 3276800 | tf_op jit(solution)/shard_map/all_gather | solution.py:24
  247.2 160.8 %all-gather.16.cloned.1.call-start = ((), (), s32[]{:S(2)}) async-start(), calls=%async_computation.16 | async-start | bytes 3686400 | tf_op jit(solution)/shard_map/all_gather | solution.py:177
  248.0 218.9 %reduce-scatter.20.cloned.1.call-start = ((), (), s32[]{:S(2)}) async-start(), calls=%async_computation.17 | async-start | bytes 6553600 | tf_op jit(solution)/shard_map/reduce_scatter | solution.py:28
  353.9 4.0 copy-start.12
  416.6 51.9 %copy-start.33 = (f32[1280]{0:T(1024)S(1)}, f32[1280]{0:T(1024)}, u32[]{:S(2)}) copy-start(f32[1280]{0:T(1024)} %param.31) | copy-start | bytes 15364
  416.6 84.3 %all-gather.18.cloned.1.call-start = ((), (), s32[]{:S(2)}) async-start(), calls=%async_computation.18 | async-start | bytes 3276800 | tf_op jit(solution)/shard_map/all_gather | solution.py:32
  466.9 3.4 copy-start.2
  466.9 3.4 copy-start.15
  475.4 85.3 %reduce-scatter.22.cloned.1.call-start = ((), (), s32[]{:S(2)}) async-start(), calls=%async_computation.19 | async-start | bytes 3276800 | tf_op jit(solution)/shard_map/reduce_scatter | solution.py:36
  513.0 1.9 copy-start.18
  525.9 67.8 %all-gather.20.cloned.1.call-start = ((), (), s32[]{:S(2)}) async-start(), calls=%async_computation.20 | async-start | bytes 3276800 | tf_op jit(solution)/shard_map/all_gather | solution.py:32
  560.7 2.0 copy-start.5
  560.7 2.3 copy-start.7
  560.7 2.5 copy-start.19
  568.2 187.6 %reduce-scatter.24.cloned.1.call-start = ((), (), s32[]{:S(2)}) async-start(), calls=%async_computation.21 | async-start | bytes 3276800 | tf_op jit(solution)/shard_map/reduce_scatter | solution.py:36
  597.6 45.8 %copy-start.32 = (f32[1024,5]{0,1:T(8,128)S(1)}, f32[1024,5]{0,1:T(8,128)}, u32[]{:S(2)}) copy-start(f32[1024,5]{0,1:T(8,128)} %copy-done.31) | copy-start | bytes 61444
  597.7 45.8 %copy-start.41 = (f32[5,64]{1,0:T(8,128)S(1)}, f32[5,64]{1,0:T(8,128)}, u32[]{:S(2)}) copy-start(f32[5,64]{1,0:T(8,128)} %copy-done.40) | copy-start | bytes 3844
  602.1 1.7 copy-start.17
  623.5 1.7 copy-start.17
  643.5 2.3 copy-start.10
  645.8 3.9 copy-start.49
  647.4 3.1 copy-start.21
  647.4 3.1 copy-start.23
  647.4 3.1 copy-start.24
  655.6 106.2 %reduce-scatter.26.cloned.1.call-start = ((), (), s32[]{:S(2)}) async-start(), calls=%async_computation.22 | async-start | bytes 2211840 | tf_op jit(solution)/shard_map/reduce_scatter | solution.py:294
  661.3 170.5 %reduce-scatter.38.cloned.1.call-start = ((), (), s32[]{:S(2)}) async-start(), calls=%async_computation.28 | async-start | bytes 2211840
  671.4 230.5 %reduce-scatter.36.cloned.1.call-start = ((), (), s32[]{:S(2)}) async-start(), calls=%async_computation.27 | async-start | bytes 2211840
  674.2 297.7 %reduce-scatter.34.cloned.1.call-start = ((), (), s32[]{:S(2)}) async-start(), calls=%async_computation.26 | async-start | bytes 2211840
  676.1 420.5 %reduce-scatter.32.cloned.1.call-start = ((), (), s32[]{:S(2)}) async-start(), calls=%async_computation.25 | async-start | bytes 7372800 | tf_op jit(solution)/shard_map/reduce_scatter | solution.py:237
  685.2 536.4 %reduce-scatter.30.cloned.1.call-start = ((), (), s32[]{:S(2)}) async-start(), calls=%async_computation.24 | async-start | bytes 7372800 | tf_op jit(solution)/shard_map/reduce_scatter | solution.py:236
  708.8 637.5 %reduce-scatter.28.cloned.1.call-start = ((), (), s32[]{:S(2)}) async-start(), calls=%async_computation.23 | async-start | bytes 7372800 | tf_op jit(solution)/shard_map/reduce_scatter | solution.py:235
  709.6 2.6 copy-start.1
  710.5 1.8 copy-start.4
  (24 other events, 27.5 us)
Sparse Core Ops, SparseCore 0:
  11.0 28.2 all-gather.7
  190.1 52.3 reduce-scatter.17
  416.8 50.0 reduce-scatter.19
  526.0 34.6 reduce-scatter.21
Sparse Core Ops, SparseCore 1:
  192.9 62.4 all-gather.11
  257.6 60.1 all-gather.13
  319.9 24.1 all-gather.9
  346.5 61.5 all-gather.15
  475.5 25.4 all-gather.17
  568.3 25.4 all-gather.19
  655.7 34.5 reduce-scatter.23
  694.2 67.5 reduce-scatter.25
  766.2 65.6 reduce-scatter.37
  835.9 65.8 reduce-scatter.35
  906.2 65.7 reduce-scatter.33
  976.1 120.4 reduce-scatter.31
  1101.1 120.5 reduce-scatter.29
  1225.8 120.5 reduce-scatter.27
where the time goes:
time: 1370 us; the launch traced here: 1360 us
  waiting for transfers between devices  886 us (65%)
  blocking collectives  199 us (15%)
  matrix products  131 us (10%)
  local copies, waits for them, and re-layouts  55.7 us (4%)
  other arithmetic  53.6 us (4%)
  between operations  20.5 us (1%)
    unnamed x21, waiting for transfers between devices  213 us
    reduce_scatter x1, waiting for transfers between devices, on_device(): lax.psum_scatter(grad_w_pair[:, ff_local:], 'dp', scatter_dimension=0, ti...  125 us
    reduce_scatter x1, waiting for transfers between devices, on_device(): lax.psum_scatter(grad_w_pair[:, :ff_local], 'dp', scatter_dimension=0, ti...  125 us
    reduce_scatter x1, waiting for transfers between devices, on_device(): lax.psum_scatter(grad_down, 'dp', scatter_dimension=1, tiled=True)  125 us
    reduce_scatter x2, waiting for transfers between devices, scatter_branch(): lax.psum_scatter(partial_sum, 'tensor', scatter_dimension=1, tiled=True)  79.6 us
    all_gather x1, waiting for transfers between devices, on_device(): lax.all_gather(w_gate, 'dp', axis=0, tiled=True)  58.6 us
    all_gather x1, waiting for transfers between devices, on_device(): lax.all_gather(w_down, 'dp', axis=1, tiled=True)  47.4 us
    all_gather x2, waiting for transfers between devices, gather_branch_grad(): return lax.all_gather(values, 'tensor', axis=1, tiled=True)  47.3 us
  transfers between devices with their start and end apart: 18, of which 16 were waited for; matrix products, arithmetic and copies ran while one was open for 7% of the time, Pallas kernels for 0%

commit v1 on v0

v1 whole, which is shorter than its diff:
```python
import math

import jax
import jax.numpy as jnp
from jax import lax
from jax.sharding import PartitionSpec as P

HEAD = 64


EPSILON = 1e-06


def normalize(vector):
    factor = lax.rsqrt(jnp.sum(vector * vector, axis=-1, keepdims=True) + EPSILON)
    return (vector * factor, factor)


def norm_back(cotangent, normed, factor):
    return factor * (cotangent - normed * jnp.sum(cotangent * normed, axis=-1, keepdims=True))


BF16 = jnp.bfloat16
F32 = jnp.float32


def ring_order(size):
    return list(range(0, size, 2)) + list(range(size - 1, 0, -2))


def ring_steps(size):
    order = ring_order(size)
    ahead = [(order[i], order[(i + 1) % size]) for i in range(size)]
    return ahead, [(b, a) for a, b in ahead]


def ring_block(size, offset):
    order = ring_order(size)
    place = [order.index(i) for i in range(size)]
    target = [order[(place[i] + offset) % size] for i in range(size)]
    return jnp.asarray(target, jnp.int32)[lax.axis_index("dp")]


def use_ring(size):
    return size % 2 == 0 and size <= 16


def ring_gather(shard):
    size = lax.axis_size("dp")
    if not use_ring(size):
        return lax.all_gather(shard, "dp", axis=0, tiled=True)
    ahead, back = ring_steps(size)
    rows, cols = shard.shape
    half = cols // 2
    full = jnp.zeros((rows * size, cols), shard.dtype)
    full = lax.dynamic_update_slice(full, shard, (lax.axis_index("dp") * rows, 0))
    fore, hind = shard, shard
    for step in range(1, size // 2):
        fore = lax.ppermute(fore, "dp", ahead)
        hind = lax.ppermute(hind, "dp", back)
        full = lax.dynamic_update_slice(full, fore, (ring_block(size, -step) * rows, 0))
        full = lax.dynamic_update_slice(full, hind, (ring_block(size, step) * rows, 0))
    fore = lax.ppermute(fore[:, :half], "dp", ahead)
    hind = lax.ppermute(hind[:, half:], "dp", back)
    far = ring_block(size, size // 2) * rows
    full = lax.dynamic_update_slice(full, fore, (far, 0))
    return lax.dynamic_update_slice(full, hind, (far, half))


def ring_reduce(partial):
    size = lax.axis_size("dp")
    if not use_ring(size):
        return lax.psum_scatter(partial, "dp", scatter_dimension=0, tiled=True).astype(F32)
    ahead, back = ring_steps(size)
    rows, cols = partial.shape[0] // size, partial.shape[1]
    half = cols // 2

    def block(offset):
        return lax.dynamic_slice(partial, (ring_block(size, offset) * rows, 0), (rows, cols))

    def total(mine, came):
        return (mine.astype(F32) + came.astype(F32)).astype(BF16)

    far = size // 2
    fore = lax.ppermute(block(far)[:, :half], "dp", ahead)
    hind = lax.ppermute(block(far)[:, half:], "dp", back)
    for step in range(far - 1, 0, -1):
        mine_fore, mine_hind = block(step), block(-step)
        if step == far - 1:
            fore = jnp.concatenate(
                [total(mine_fore[:, :half], fore), mine_fore[:, half:]], axis=1
            )
            hind = jnp.concatenate(
                [mine_hind[:, :half], total(mine_hind[:, half:], hind)], axis=1
            )
        else:
            fore, hind = total(mine_fore, fore), total(mine_hind, hind)
        fore = lax.ppermute(fore, "dp", ahead)
        hind = lax.ppermute(hind, "dp", back)
    return block(0).astype(F32) + fore.astype(F32) + hind.astype(F32)


def tensor_swap(values, bit):
    size = lax.axis_size("tensor")
    return lax.ppermute(values, "tensor", [(i, i ^ bit) for i in range(size)])


def gather_rows(rows):
    across = tensor_swap(rows, 2)
    beside = tensor_swap(rows, 1)
    return jnp.concatenate([rows, beside, across, tensor_swap(across, 1)], axis=0)


def scatter_rows(partial):
    count = partial.shape[0] // 4
    own, beside, across, opposite = (partial[k * count : (k + 1) * count] for k in range(4))
    across = across.astype(F32) + tensor_swap(opposite.astype(BF16), 1).astype(F32)
    across = tensor_swap(across.astype(BF16), 2)
    own = own.astype(F32) + tensor_swap(beside.astype(BF16), 1).astype(F32)
    return own + across.astype(F32)


def all_sum(values):
    dp_size = lax.axis_size("dp")
    if dp_size & (dp_size - 1) or dp_size > 16:
        return lax.psum(values, "dp")
    bit = 1
    while bit < dp_size:
        values = values + lax.ppermute(values, "dp", [(i, i ^ bit) for i in range(dp_size)])
        bit *= 2
    return values


def tensor_sum(values):
    values = values + tensor_swap(values, 1)
    return values + tensor_swap(values, 2)


def slot_order(slot_count):
    count = slot_count // 4
    index = jnp.arange(slot_count, dtype=jnp.int32)
    return ((index // count) ^ lax.axis_index("tensor")) * count + index % count


def masked_scores(query_block, k_seq, first_row, length):
    slot_count = k_seq.shape[0]
    block_rows = query_block.shape[0]
    scores = math.sqrt(query_block.shape[2]) * jnp.einsum(
        "qhd,khd->hqk", query_block, k_seq, preferred_element_type=jnp.float32
    )
    key_ids = slot_order(slot_count).reshape(1, slot_count)
    query_ids = lax.dynamic_slice_in_dim(slot_order(slot_count), first_row, block_rows).reshape(
        block_rows, 1
    )
    allowed = (key_ids <= query_ids) & (key_ids < length)
    return jnp.where(allowed[None], scores, -1e30)


def attend(q_seq, k_seq, v_seq, length, block_rows):
    slot_count = q_seq.shape[0]

    def one_block(first_row):
        query_block = lax.dynamic_slice_in_dim(q_seq, first_row, block_rows, 0)
        scores = masked_scores(query_block, k_seq, first_row, length)
        row_max = jnp.max(scores, axis=-1, keepdims=True)
        exponent = jnp.exp(scores - row_max)
        row_total = jnp.sum(exponent, axis=-1, keepdims=True)
        probabilities = (exponent / row_total).astype(jnp.bfloat16)
        block_out = jnp.einsum(
            "hqk,khd->qhd", probabilities, v_seq, preferred_element_type=jnp.float32
        )
        return (block_out, (row_max + jnp.log(row_total))[..., 0])

    starts = jnp.arange(slot_count // block_rows, dtype=jnp.int32) * block_rows
    block_outs, log_totals = lax.map(one_block, starts)
    return (block_outs.reshape(q_seq.shape), log_totals)


def attend_back(q_seq, k_seq, v_seq, log_totals, grad_seq, length, block_rows):
    slot_count = q_seq.shape[0]
    root_scale = math.sqrt(q_seq.shape[2])

    def one_block(running, block_item):
        first_row, block_totals = block_item
        grad_keys, grad_values = running
        query_block = lax.dynamic_slice_in_dim(q_seq, first_row, block_rows, 0)
        grad_block = lax.dynamic_slice_in_dim(grad_seq, first_row, block_rows, 0)
        scores = masked_scores(query_block, k_seq, first_row, length)
        probabilities = jnp.exp(scores - block_totals[..., None])
        grad_probs = jnp.einsum(
            "qhd,khd->hqk", grad_block, v_seq, preferred_element_type=jnp.float32
        )
        row_delta = jnp.sum(grad_probs * probabilities, axis=-1, keepdims=True)
        grad_scores = (probabilities * (grad_probs - row_delta)).astype(jnp.bfloat16)
        grad_query = root_scale * jnp.einsum(
            "hqk,khd->qhd", grad_scores, k_seq, preferred_element_type=jnp.float32
        )
        grad_keys = grad_keys + root_scale * jnp.einsum(
            "hqk,qhd->khd", grad_scores, query_block, preferred_element_type=jnp.float32
        )
        grad_values = grad_values + jnp.einsum(
            "hqk,qhd->khd",
            probabilities.astype(jnp.bfloat16),
            grad_block,
            preferred_element_type=jnp.float32,
        )
        return ((grad_keys, grad_values), grad_query)

    starts = jnp.arange(slot_count // block_rows, dtype=jnp.int32) * block_rows
    zeros_kv = jnp.zeros(q_seq.shape, jnp.float32)
    (grad_keys, grad_values), grad_queries = lax.scan(
        one_block, (zeros_kv, zeros_kv), (starts, log_totals)
    )
    return (grad_queries.reshape(q_seq.shape), grad_keys, grad_values)


def on_device(
    hidden_in,
    lengths,
    teacher,
    w_query,
    w_key,
    w_value,
    w_attn_out,
    w_up,
    w_gate,
    w_down,
    s_qk,
    alpha_attn,
    alpha_mlp,
    s_up,
    s_gate,
):
    tensor_rank = lax.axis_index("tensor")
    seq_count, local_slots, model_width = hidden_in.shape
    slot_count = local_slots * lax.axis_size("tensor")
    heads_width = w_query.shape[1]
    head_count = heads_width // HEAD
    ff_local = w_up.shape[1]
    block_rows = min(512, slot_count)
    gate_root = math.sqrt(model_width)
    total_slots = slot_count * seq_count * lax.axis_size("dp")
    hidden = hidden_in.reshape(local_slots, model_width)
    teacher = teacher.reshape(local_slots, model_width)
    length = lengths[0]
    w_project = ring_gather(jnp.concatenate([w_query, w_key, w_value], axis=1))
    w_out = ring_gather(w_attn_out.T)
    token_count = all_sum(lengths.astype(F32))[0]
    stream = gather_rows(hidden.astype(BF16))
    projected = jnp.dot(stream, w_project, preferred_element_type=F32)
    q_raw = projected[:, :heads_width].reshape(slot_count, head_count, HEAD)
    k_raw = projected[:, heads_width : 2 * heads_width].reshape(slot_count, head_count, HEAD)
    v_low = projected[:, 2 * heads_width :].astype(BF16).reshape(slot_count, head_count, HEAD)
    q_unit, q_factor = normalize(q_raw)
    k_unit, k_factor = normalize(k_raw)
    qk_gain = lax.dynamic_slice_in_dim(s_qk, tensor_rank * heads_width, heads_width).reshape(
        head_count, HEAD
    )
    q_low = (q_unit * qk_gain).astype(BF16)
    k_low = (k_unit * qk_gain).astype(BF16)
    attended, log_totals = attend(q_low, k_low, v_low, length, block_rows)
    attended_low = attended.reshape(slot_count, heads_width).astype(BF16)
    attn_part = jnp.einsum("rc,dc->rd", attended_low, w_out, preferred_element_type=F32)
    attn_sum = scatter_rows(attn_part)
    attn_unit, attn_factor = normalize(attn_sum)
    first_out, first_factor = normalize(hidden + alpha_attn * (attn_unit - hidden))
    w_pair = ring_gather(jnp.concatenate([w_up, w_gate], axis=1))
    w_low = ring_gather(w_down.T)
    mlp_in = gather_rows(first_out.astype(BF16))
    up_gate = jnp.dot(mlp_in, w_pair, preferred_element_type=F32)
    up_raw = up_gate[:, :ff_local]
    gate_raw = up_gate[:, ff_local:]
    up_gain = lax.dynamic_slice_in_dim(s_up, tensor_rank * ff_local, ff_local)
    gate_gain = lax.dynamic_slice_in_dim(s_gate, tensor_rank * ff_local, ff_local) * gate_root
    scaled_up = up_raw * up_gain
    scaled_gate = gate_raw * gate_gain
    sigmoid_gate = jax.nn.sigmoid(scaled_gate)
    activated = scaled_gate * sigmoid_gate
    hidden_low = (scaled_up * activated).astype(BF16)
    mlp_part = jnp.einsum("rf,df->rd", hidden_low, w_low, preferred_element_type=F32)
    mlp_sum = scatter_rows(mlp_part)
    mlp_unit, mlp_factor = normalize(mlp_sum)
    output, out_factor = normalize(first_out + alpha_mlp * (mlp_unit - first_out))
    slot_ids = tensor_rank * local_slots + lax.broadcasted_iota(jnp.int32, (local_slots, 1), 0)
    valid_mask = (slot_ids < length).astype(F32)
    difference = output - teacher
    error_sum = jnp.sum(jnp.sum(difference * difference, axis=-1, keepdims=True) * valid_mask)
    grad_output = 2.0 * total_slots / token_count * difference * valid_mask
    grad_mixed_two = norm_back(grad_output, output, out_factor)
    grad_alpha_mlp = jnp.sum(grad_mixed_two * (mlp_unit - first_out), axis=0)
    grad_first = grad_mixed_two * (1.0 - alpha_mlp)
    grad_mlp_sum = norm_back(grad_mixed_two * alpha_mlp, mlp_unit, mlp_factor).astype(BF16)
    grad_mlp_rows = gather_rows(grad_mlp_sum)
    grad_low = jnp.einsum("rd,rf->df", grad_mlp_rows, hidden_low, preferred_element_type=F32)
    grad_w_down = ring_reduce(grad_low.astype(BF16)).T
    grad_hidden = jnp.dot(grad_mlp_rows, w_low, preferred_element_type=F32)
    grad_scaled_up = grad_hidden * activated
    grad_scaled_gate = (
        grad_hidden * scaled_up * sigmoid_gate * (1.0 + scaled_gate * (1.0 - sigmoid_gate))
    )
    grad_up_gain = jnp.sum(grad_scaled_up * up_raw, axis=0)
    grad_gate_gain = jnp.sum(grad_scaled_gate * gate_raw, axis=0) * gate_root
    grad_pair = jnp.concatenate(
        [grad_scaled_up * up_gain, grad_scaled_gate * gate_gain], axis=1
    ).astype(BF16)
    grad_mlp_in = jnp.einsum("rf,df->rd", grad_pair, w_pair, preferred_element_type=F32)
    grad_w_pair = jnp.einsum("rd,rf->df", mlp_in, grad_pair, preferred_element_type=F32)
    grad_first = grad_first + scatter_rows(grad_mlp_in)
    grad_w_pair = ring_reduce(grad_w_pair.astype(BF16))
    grad_mixed = norm_back(grad_first, first_out, first_factor)
    grad_alpha_attn = jnp.sum(grad_mixed * (attn_unit - hidden), axis=0)
    grad_input = grad_mixed * (1.0 - alpha_attn)
    grad_attn_sum = norm_back(grad_mixed * alpha_attn, attn_unit, attn_factor).astype(BF16)
    grad_attn_rows = gather_rows(grad_attn_sum)
    grad_out = jnp.einsum("rd,rc->dc", grad_attn_rows, attended_low, preferred_element_type=F32)
    grad_attended = jnp.dot(grad_attn_rows, w_out, preferred_element_type=F32)
    grad_attended = grad_attended.astype(BF16).reshape(slot_count, head_count, HEAD)
    grad_q_low, grad_k_low, grad_v_low = attend_back(
        q_low, k_low, v_low, log_totals, grad_attended, length, block_rows
    )
    grad_gain = jnp.sum(grad_q_low * q_unit + grad_k_low * k_unit, axis=0).reshape(heads_width)
    grad_q = norm_back(grad_q_low * qk_gain, q_unit, q_factor).reshape(slot_count, heads_width)
    grad_k = norm_back(grad_k_low * qk_gain, k_unit, k_factor).reshape(slot_count, heads_width)
    grad_project = jnp.concatenate(
        [grad_q, grad_k, grad_v_low.reshape(slot_count, heads_width)], axis=1
    ).astype(BF16)
    grad_w_project = jnp.einsum("rd,rc->dc", stream, grad_project, preferred_element_type=F32)
    grad_stream = jnp.einsum("rc,dc->rd", grad_project, w_project, preferred_element_type=F32)
    grad_input = grad_input + scatter_rows(grad_stream)
    grad_w_attn = ring_reduce(
        jnp.concatenate([grad_w_project, grad_out], axis=1).astype(BF16)
    )

    def placed(values):
        width = values.shape[0]
        return lax.dynamic_update_slice_in_dim(
            jnp.zeros((width * lax.axis_size("tensor"),), F32), values, tensor_rank * width, 0
        )

    vectors = jnp.concatenate(
        [
            error_sum.reshape(1),
            grad_alpha_attn,
            grad_alpha_mlp,
            placed(grad_gain),
            placed(grad_up_gain),
            placed(grad_gate_gain),
        ]
    )
    vectors = all_sum(tensor_sum(vectors))
    loss = vectors[0] / token_count
    cuts = [1 + model_width * k for k in range(4)] + [1 + 3 * model_width + s_up.shape[0]]
    return (
        loss,
        output[None],
        (grad_input)[None],
        grad_w_attn[:, :heads_width],
        grad_w_attn[:, heads_width : 2 * heads_width],
        grad_w_attn[:, 2 * heads_width : 3 * heads_width],
        grad_w_attn[:, 3 * heads_width :].T,
        grad_w_pair[:, :ff_local],
        grad_w_pair[:, ff_local:],
        grad_w_down,
        vectors[cuts[2] : cuts[3]],
        vectors[cuts[0] : cuts[1]],
        vectors[cuts[1] : cuts[2]],
        vectors[cuts[3] : cuts[4]],
        vectors[cuts[4] :],
    )


def solution(mesh):
    in_specs = (
        P("dp", "tensor", None),
        P("dp"),
        P("dp", "tensor", None),
        P("dp", "tensor"),
        P("dp", "tensor"),
        P("dp", "tensor"),
        P("tensor", "dp"),
        P("dp", "tensor"),
        P("dp", "tensor"),
        P("tensor", "dp"),
        P(),
        P(),
        P(),
        P(),
        P(),
    )
    out_specs = (
        P(),
        P("dp", "tensor", None),
        P("dp", "tensor", None),
        P("dp", "tensor"),
        P("dp", "tensor"),
        P("dp", "tensor"),
        P("tensor", "dp"),
        P("dp", "tensor"),
        P("dp", "tensor"),
        P("tensor", "dp"),
        P(),
        P(),
        P(),
        P(),
        P(),
    )
    return jax.shard_map(
        on_device, mesh=mesh, in_specs=in_specs, out_specs=out_specs, check_vma=False
    )
```

time: 1370 us -> 580 us (0.42)
  waiting for transfers between devices: 886 us -> 185 us
  blocking collectives: 199 us -> 0 us
  starting transfers between devices: 1.64 us -> 82.8 us
  local copies, waits for them, and re-layouts: 55.7 us -> 94.5 us
    reduce_scatter x8 -> x0, waiting for transfers between devices: 492 us -> none  [the longest x1 125 us: on_device(): lax.psum_scatter(grad_w_pair[:, ff_local:], 'dp', scatter_dimension=0, ti...]
    unnamed x21 -> x0, waiting for transfers between devices: 213 us -> none
    ppermute x0 -> x88, waiting for transfers between devices: none -> 185 us  [the longest x9 44.9 us: ring_reduce(): fore = lax.ppermute(fore, 'dp', ahead)]
    all_gather x7 -> x0, waiting for transfers between devices: 181 us -> none  [the longest x1 58.6 us: on_device(): lax.all_gather(w_gate, 'dp', axis=0, tiled=True)]
    all_gather x4 -> x0, blocking collectives: 137 us -> none  [the longest x1 35 us: on_device(): lax.all_gather(w_attn_out, 'dp', axis=1, tiled=True)]
    ppermute x0 -> x88, starting transfers between devices: none -> 82.8 us  [the longest x12 21.2 us: ring_gather(): fore = lax.ppermute(fore, 'dp', ahead)]
    psum x2 -> x0, blocking collectives: 61.7 us -> none  [the longest x1 41.4 us: on_device(): lax.psum((error_sum, grad_alpha_attn, grad_alpha_mlp, full_gain, full_up,...]
    dynamic_update_slice x2 -> x37, local copies, waits for them, and re-layouts: 0.47 us -> 44.4 us  [the longest x12 14.9 us: ring_gather(): lax.dynamic_update_slice(full, fore, (ring_block(size, -step) * rows, 0))]
  transfers between devices with their start and end apart: 18 -> 88, of which waited for: 16 -> 38; matrix products, arithmetic and copies ran while one was open for 7% -> 41% of each run, Pallas kernels for 0% -> 0%
where the time goes in v1:
time: 580 us; the launch traced here: 572 us
  waiting for transfers between devices  185 us (32%)
  matrix products  129 us (22%)
  local copies, waits for them, and re-layouts  94.5 us (16%)
  starting transfers between devices  82.8 us (14%)
  other arithmetic  61.4 us (11%)
  between operations  11 us (2%)
  loops' own time  8.22 us (1%)
    ppermute x9, waiting for transfers between devices, ring_reduce(): fore = lax.ppermute(fore, 'dp', ahead)  44.9 us
    ppermute x26, waiting for transfers between devices, tensor_swap(): return lax.ppermute(values, 'tensor', [(i, i ^ bit) for i in range(size)])  44.5 us
    ppermute x12, waiting for transfers between devices, ring_gather(): hind = lax.ppermute(hind, 'dp', back)  30.7 us
    ppermute x12, starting transfers between devices, ring_gather(): fore = lax.ppermute(fore, 'dp', ahead)  21.2 us
    ppermute x6, waiting for transfers between devices, all_sum(): lax.ppermute(values, 'dp', [(i, i ^ bit) for i in range(dp_size)])  20 us
    ppermute x9, waiting for transfers between devices, ring_reduce(): hind = lax.ppermute(hind, 'dp', back)  16.9 us
    ppermute x12, waiting for transfers between devices, ring_gather(): fore = lax.ppermute(fore, 'dp', ahead)  16.8 us
    dynamic_update_slice x12, local copies, waits for them, and re-layouts, ring_gather(): lax.dynamic_update_slice(full, fore, (ring_block(size, -step) * rows, 0))  14.9 us
  transfers between devices with their start and end apart: 88, of which 38 were waited for; matrix products, arithmetic and copies ran while one was open for 41% of the time, Pallas kernels for 0%

profile of v1, /device:TPU:0, one launch (start us, length us, event | category | flops | bytes accessed | tf_op | source)
XLA Modules:
  0.0 572.1 jit_solution(9385744325674230499)
XLA Ops:
  39.2 7.4 %collective-permute-done.13 = bf16[160,320]{1,0:T(8,128)(2,1)S(1)} collective-permute-done((bf16[160,320]{1,0:T(8,128)(2,1)}, bf16[160,320]{1,0:T(8,128)(2,1)S(1)}, u32[]{:S(2)}, u32[]{:S(2)}) %collective-permute-start.13) | collective-permute-done | bytes 102432 | tf_op jit(solution)/shard_map/ppermute | solution.py:59
  47.8 3.9 collective-permute-done.14
  76.5 5.8 %collective-permute-done.6 = bf16[160,960]{1,0:T(8,128)(2,1)S(1)} collective-permute-done((bf16[160,960]{1,0:T(8,128)(2,1)}, bf16[160,960]{1,0:T(8,128)(2,1)S(1)}, u32[]{:S(2)}, u32[]{:S(2)}) %collective-permute-start.6) | collective-permute-done | bytes 307232 | tf_op jit(solution)/shard_map/ppermute | solution.py:60
  87.9 5.6 collective-permute-done.35
  94.1 19.2 %collective-permute-done.8 = bf16[160,960]{1,0:T(8,128)(2,1)S(1)} collective-permute-done((bf16[160,960]{1,0:T(8,128)(2,1)S(1)}, bf16[160,960]{1,0:T(8,128)(2,1)S(1)}, u32[]{:S(2)}, u32[]{:S(2)}) %collective-permute-start.8) | collective-permute-done | bytes 307232 | tf_op jit(solution)/shard_map/ppermute | solution.py:60
  125.5 3.4 dynamic_update_slice.145
  131.7 5.2 fusion.87
  140.4 26.8 %while.33 = (s32[]{:T(128)}, bf16[2,512,5,64]{1,3,2,0:T(8,128)(2,1)}, f32[2,5,512]{2,1,0:T(8,128)S(1)}, s32[2]{0:T(128)S(1)}, s32[]{:T(128)}, /*index=5*/bf16[10...) while((s32[]{:T(128)}, ...), condition=%wide.region_5.6_spmd.clone, body=%wide.region_2.5_spmd.sunk.clone | while | flops 703623680 | bytes 35965612 | solution.py:175
  149.5 4.3 fusion.187
  162.9 4.3 fusion.187
  180.1 3.4 collective-permute-done.39
  190.9 9.0 %collective-permute-done.21 = bf16[256,1280]{1,0:T(8,128)(2,1)S(1)} collective-permute-done((bf16[256,1280]{1,0:T(8,128)(2,1)S(1)}, bf16[256,1280]{1,0:T(8,128)(2,1)S(1)}, u32[]{:S(2)}, u32[]{:S(2)}) %collective-permute-start.21) | collective-permute-done | bytes 655392 | tf_op jit(solution)/shard_map/ppermute | solution.py:105
  209.7 7.0 %collective-permute-done.23 = bf16[256,1280]{1,0:T(8,128)(2,1)S(1)} collective-permute-done((bf16[256,1280]{1,0:T(8,128)(2,1)S(1)}, bf16[256,1280]{1,0:T(8,128)(2,1)S(1)}, u32[]{:S(2)}, u32[]{:S(2)}) %collective-permute-start.23) | collective-permute-done | bytes 655392 | tf_op jit(solution)/shard_map/ppermute | solution.py:105
  219.4 9.6 %fusion.86 = f32[1024,2560]{1,0:T(8,128)S(1)} fusion(bf16[1280,2560]{1,0:T(8,128)(2,1)} %constant_dynamic-update-slice_fusion.33, bf16[256,1280]{1,0:T(8,128)(2,1)S(1)} %collective-permute-done.24, bf16[256,1280]{1,0:T(8,128)(2,1)S(1)} %collective-permute-done.23, bf16[256,1280]{1,0:T(8,128)(2,1)S(1)} %collective-permute-done.22, ...), kind=kOutput, calls=%fused_computation.200 | convolution fusion | flops 6721372160 | bytes 19660800 | tf_op jit(solution)/shard_map/dot_general | solution.py:270
  232.9 6.5 %fusion.120 = (bf16[1024,1280]{1,0:T(8,128)(2,1)S(1)}, f32[1024,1280]{1,0:T(8,128)S(1)}) fusion(bf16[1024,1280]{1,0:T(8,128)(2,1)S(1)} %multiply_convert_fusion.3, bf16[1280,1280]{1,0:T(8,128)(2,1)} %constant_dynamic-update-slice_fusion.32), kind=kOutput, calls=%fused_computation.292 | convolution fusion | flops 3356753920 | bytes 13762560 | tf_op jit(solution)/shard_map/rf,df->rd/dot_general | solution.py:280
  253.3 4.0 collective-permute-start.46
  269.2 16.2 %collective-permute-done.48 = bf16[256,1280]{1,0:T(8,128)(2,1)} collective-permute-done((bf16[256,1280]{1,0:T(8,128)(2,1)}, bf16[256,1280]{1,0:T(8,128)(2,1)}, u32[]{:S(2)}, u32[]{:S(2)}) %collective-permute-start.48) | collective-permute-done | bytes 655392 | tf_op jit(solution)/shard_map/ppermute | solution.py:105
  286.0 3.2 reshape.446
  289.9 6.4 %convolution_convert_fusion.1 = bf16[1280,1280]{1,0:T(8,128)(2,1)S(1)} fusion(bf16[1024,1280]{1,0:T(8,128)(2,1)} %copy-done.32, bf16[256,1280]{1,0:T(8,128)(2,1)} %collective-permute-done.49, bf16[256,1280]{1,0:T(8,128)(2,1)} %collective-permute-done.48, bf16[256,1280]{1,0:T(8,128)(2,1)} %collective-permute-done.47, ...), kind=kOutput, calls=%fused_computation.83 | convolution fusion | flops 3367567360 | bytes 8519680 | tf_op jit(solution)/shard_map/rd,rf->df/dot_general | solution.py:294
  299.3 11.1 %multiply_reduce_fusion.1 = (f32[1280]{0:T(1024)S(1)}, f32[1280]{0:T(1024)S(1)}, f32[1024,1280]{1,0:T(8,128)S(1)}, bf16[1024,1280]{1,0:T(8,128)(2,1)}) fusion(f32[1024,2560]{1,0:T(8,128)S(1)} %bitcast.177, f32[1280]{0:T(1024)S(1)} %dynamic-slice_multiply_fusion, f32[1280]{0:T(1024)S(1)} %dynamic_slice.327, ...), kind=kOutput, calls=%fused_computation.85 | convolution fusion | flops 3390830080 | bytes 24268800 | tf_op jit(solution)/shard_map/dot_general | solution.py:296
  312.2 11.7 %fusion.121 = (bf16[1024,1280]{1,0:T(8,128)(2,1)S(1)}, f32[1024,1280]{1,0:T(8,128)}) fusion(bf16[1280,2560]{1,0:T(8,128)(2,1)} %constant_dynamic-update-slice_fusion.33, bf16[1024,1280]{1,0:T(8,128)(2,1)S(1)} %multiply_convert_fusion.1, bf16[1024,1280]{1,0:T(8,128)(2,1)S(1)} %copy-done.80), kind=kOutput, calls=%fused_computation.293 | convolution fusion | flops 6722682880 | bytes 19660800 | tf_op jit(solution)/shard_map/rf,df->rd/dot_general | solution.py:306
  324.0 7.4 %convolution_convert_fusion = bf16[1280,2560]{1,0:T(8,128)(2,1)S(1)} fusion(bf16[1024,1280]{1,0:T(8,128)(2,1)S(1)} %multiply_convert_fusion.1, bf16[1024,1280]{1,0:T(8,128)(2,1)S(1)} %copy-done.81, bf16[256,1280]{1,0:T(8,128)(2,1)S(1)} %copy-done.65, bf16[256,1280]{1,0:T(8,128)(2,1)S(1)} %copy-done.61, bf16[256,1280]{1,0:T(8,128)(2,1)S(1)} %copy-done.63, ...), kind=kOutput, calls=%fused_computation.74 | convolution fusion | flops 6735134720 | bytes 14417920 | tf_op jit(solution)/shard_map/rd,rf->df/dot_general | solution.py:307
  343.5 3.2 collective-permute-done.72
  351.6 5.6 collective-permute-done.81
  362.1 22.2 %collective-permute-done.82 = bf16[160,1280]{1,0:T(8,128)(2,1)S(1)} collective-permute-done((bf16[160,1280]{1,0:T(8,128)(2,1)S(1)}, bf16[160,1280]{1,0:T(8,128)(2,1)S(1)}, u32[]{:S(2)}, u32[]{:S(2)}) %collective-permute-start.82) | collective-permute-done | bytes 409632 | tf_op jit(solution)/shard_map/ppermute | solution.py:98
  398.5 3.5 collective-permute-done.87
  403.1 5.5 collective-permute-done.54
  408.6 3.7 collective-permute-done.74
  417.3 4.5 convolution_convert_fusion.4
  421.8 57.0 %while.34 = (s32[]{:T(128)}, f32[1024,5,64]{0,2,1:T(8,128)S(1)}, f32[1024,5,64]{0,2,1:T(8,128)}, f32[2,512,5,64]{1,3,2,0:T(8,128)}, s32[2]{0:T(128)S(1)}, /*inde...) while((s32[]{:T(128)}, f32[1024,5,64]{0,2,1:T(8,128)S(1)}, ...), condition=%wide.region_20.21_spmd.clone.clone, body=%wide.region_18.20_spmd.clone.sunk.clone | while | flops 1719923200 | bytes 181767024 | solution.py:211
  427.3 4.1 multiply_reduce_fusion.19
  431.3 4.5 multiply_convert_fusion.11
  435.8 3.9 fusion.199
  439.7 5.7 %fusion.201 = f32[2,512,5,64]{1,3,2,0:T(8,128)} fusion(f32[2,512,5,64]{1,3,2,0:T(8,128)} %get-tuple-element.687, s32[]{:T(128)} %get-tuple-element.684, bf16[5,512,1024]{2,1,0:T(8,128)(2,1)} %multiply_convert_fusion.11, bf16[1024,5,64]{0,2,1:T(8,128)(2,1)S(1)} %get-tuple-element.702), kind=kOutput, calls=%fused_computation.44.clone.1.clone | convolution fusion | flops 335708160 | bytes 6554112 | tf_op jit(solution)/shard_map/while/body/eval_jaxpr/hqk,khd->qhd/dot_general | solution.py:195
  445.4 4.2 fusion.200
  455.0 4.1 multiply_reduce_fusion.19
  459.1 4.5 multiply_convert_fusion.11
  463.5 3.9 fusion.199
  467.4 5.7 fusion.201
  473.1 5.5 fusion.200
  492.6 4.9 fusion.122
  499.4 4.4 convolution_convert_fusion.2
  510.3 4.2 collective-permute-done.58
  515.4 4.0 collective-permute-done.59
  522.5 9.3 %collective-permute-done.60 = f32[14081]{0:T(1024)S(1)} collective-permute-done((f32[14081]{0:T(1024)S(1)}, f32[14081]{0:T(1024)S(1)}, u32[]{:S(2)}, u32[]{:S(2)}) %collective-permute-start.60) | collective-permute-done | bytes 56356 | tf_op jit(solution)/shard_map/ppermute | solution.py:129
  536.4 4.7 collective-permute-done.65
  543.6 5.8 %collective-permute-done.66 = bf16[160,1280]{1,0:T(8,128)(2,1)S(1)} collective-permute-done((bf16[160,1280]{1,0:T(8,128)(2,1)S(1)}, bf16[160,1280]{1,0:T(8,128)(2,1)S(1)}, u32[]{:S(2)}, u32[]{:S(2)}) %collective-permute-start.66) | collective-permute-done | bytes 409632 | tf_op jit(solution)/shard_map/ppermute | solution.py:98
  550.9 10.2 %collective-permute-done.70 = bf16[160,1280]{1,0:T(8,128)(2,1)S(1)} collective-permute-done((bf16[160,1280]{1,0:T(8,128)(2,1)S(1)}, bf16[160,1280]{1,0:T(8,128)(2,1)S(1)}, u32[]{:S(2)}, u32[]{:S(2)}) %collective-permute-start.70) | collective-permute-done | bytes 409632 | tf_op jit(solution)/shard_map/ppermute | solution.py:99
  (525 shorter events, 256.4 us)
Async XLA Ops:
  3.6 49.8 %collective-permute-start.3 = (bf16[160,960]{1,0:T(8,128)(2,1)}, bf16[160,960]{1,0:T(8,128)(2,1)}, u32[]{:S(2)}, u32[]{:S(2)}) collective-permute-start(bf16[160,960]{1,0:T(8,128)(2,1)} %get-tuple-element.408), channel_id=1, source_target_pairs={{0,8},{8,16},{16,24},{24,28},{28,20},{20,12},{12,4},{4,0},{1,9},{9... | collective-permute-start | bytes 921608 | tf_op jit(solution)/shard_map/ppermute | solution.py:59
  6.6 54.7 %collective-permute-start.4 = (bf16[160,960]{1,0:T(8,128)(2,1)}, bf16[160,960]{1,0:T(8,128)(2,1)}, u32[]{:S(2)}, u32[]{:S(2)}) collective-permute-start(bf16[160,960]{1,0:T(8,128)(2,1)} %get-tuple-element.408), channel_id=1, source_target_pairs={{8,0},{16,8},{24,16},{28,24},{20,28},{12,20},{4,12},{0,4},{9,1},{1... | collective-permute-start | bytes 921608 | tf_op jit(solution)/shard_map/ppermute | solution.py:60
  6.6 26.9 %collective-permute-start.11 = (bf16[160,320]{1,0:T(8,128)(2,1)}, bf16[160,320]{1,0:T(8,128)(2,1)S(1)}, u32[]{:S(2)}, u32[]{:S(2)}) collective-permute-start(bf16[160,320]{1,0:T(8,128)(2,1)} %bitcast.16), channel_id=1, source_target_pairs={{0,8},{8,16},{16,24},{24,28},{28,20},{20,12},{12,4},{4,0},{1,9},{9... | collective-permute-start | bytes 307208 | tf_op jit(solution)/shard_map/ppermute | solution.py:59
  8.6 28.1 %collective-permute-start.12 = (bf16[160,320]{1,0:T(8,128)(2,1)}, bf16[160,320]{1,0:T(8,128)(2,1)}, u32[]{:S(2)}, u32[]{:S(2)}) collective-permute-start(bf16[160,320]{1,0:T(8,128)(2,1)} %bitcast.16), channel_id=1, source_target_pairs={{8,0},{16,8},{24,16},{28,24},{20,28},{12,20},{4,12},{0,4},{9,1},{1... | collective-permute-start | bytes 307208 | tf_op jit(solution)/shard_map/ppermute | solution.py:60
  10.2 74.9 %collective-permute-start.25 = (bf16[160,2560]{1,0:T(8,128)(2,1)}, bf16[160,2560]{1,0:T(8,128)(2,1)}, u32[]{:S(2)}, u32[]{:S(2)}) collective-permute-start(bf16[160,2560]{1,0:T(8,128)(2,1)} %constant_dynamic-update-slice_fusion.30), channel_id=1, source_target_pairs={{0,8},{8,16},{16,24},{24,28},{28,20},{20,12},{12,4},{4,0},{1,9},{9... | collective-permute-start | bytes 2457608 | tf_op jit(solution)/shard_map/ppermute | solution.py:59
  34.2 36.5 %collective-permute-start.33 = (bf16[160,1280]{1,0:T(8,128)(2,1)S(1)}, bf16[160,1280]{1,0:T(8,128)(2,1)S(1)}, u32[]{:S(2)}, u32[]{:S(2)}) collective-permute-start(bf16[160,1280]{1,0:T(8,128)(2,1)S(1)} %bitcast.188), channel_id=1, source_target_pairs={{0,8},{8,16},{16,24},{24,28},{28,20},{20,12},{12,4},{4,0},{1,9},{9... | collective-permute-start | bytes 1228808 | tf_op jit(solution)/shard_map/ppermute | solution.py:59
  56.6 15.1 %collective-permute-start.34 = (bf16[160,1280]{1,0:T(8,128)(2,1)S(1)}, bf16[160,1280]{1,0:T(8,128)(2,1)S(1)}, u32[]{:S(2)}, u32[]{:S(2)}) collective-permute-start(bf16[160,1280]{1,0:T(8,128)(2,1)S(1)} %bitcast.189), channel_id=1, source_target_pairs={{8,0},{16,8},{24,16},{28,24},{20,28},{12,20},{4,12},{0,4},{9,1},{1... | collective-permute-start | bytes 1228808 | tf_op jit(solution)/shard_map/ppermute | solution.py:60
  67.5 17.3 %collective-permute-start.1 = (bf16[256,1280]{1,0:T(8,128)(2,1)S(1)}, bf16[256,1280]{1,0:T(8,128)(2,1)}, u32[]{:S(2)}, u32[]{:S(2)}) collective-permute-start(bf16[256,1280]{1,0:T(8,128)(2,1)S(1)} %bitcast_convert_fusion), channel_id=1, source_target_pairs={{0,2},{1,3},{2,0},{3,1},{4,6},{5,7},{6,4},{7,5},{8,10},{9,11},{10,... | collective-permute-start | bytes 1966088 | tf_op jit(solution)/shard_map/ppermute | solution.py:105
  70.7 58.3 %collective-permute-start = (bf16[256,1280]{1,0:T(8,128)(2,1)S(1)}, bf16[256,1280]{1,0:T(8,128)(2,1)}, u32[]{:S(2)}, u32[]{:S(2)}) collective-permute-start(bf16[256,1280]{1,0:T(8,128)(2,1)S(1)} %bitcast_convert_fusion), channel_id=1, source_target_pairs={{0,1},{1,0},{2,3},{3,2},{4,5},{5,4},{6,7},{7,6},{8,9},{9,8},{10,11... | collective-permute-start | bytes 1966088 | tf_op jit(solution)/shard_map/ppermute | solution.py:105
  72.9 13.0 %collective-permute-start.7 = (bf16[160,960]{1,0:T(8,128)(2,1)}, bf16[160,960]{1,0:T(8,128)(2,1)S(1)}, u32[]{:S(2)}, u32[]{:S(2)}) collective-permute-start(bf16[160,960]{1,0:T(8,128)(2,1)} %collective-permute-done.5), channel_id=1, source_target_pairs={{0,8},{8,16},{16,24},{24,28},{28,20},{20,12},{12,4},{4,0},{1,9},{9... | collective-permute-start | bytes 921608 | tf_op jit(solution)/shard_map/ppermute | solution.py:59
  84.9 45.6 %collective-permute-start.26 = (bf16[160,2560]{1,0:T(8,128)(2,1)}, bf16[160,2560]{1,0:T(8,128)(2,1)}, u32[]{:S(2)}, u32[]{:S(2)}) collective-permute-start(bf16[160,2560]{1,0:T(8,128)(2,1)} %constant_dynamic-update-slice_fusion.30), channel_id=1, source_target_pairs={{8,0},{16,8},{24,16},{28,24},{20,28},{12,20},{4,12},{0,4},{9,1},{1... | collective-permute-start | bytes 2457608 | tf_op jit(solution)/shard_map/ppermute | solution.py:60
  85.1 28.2 %collective-permute-start.8 = (bf16[160,960]{1,0:T(8,128)(2,1)S(1)}, bf16[160,960]{1,0:T(8,128)(2,1)S(1)}, u32[]{:S(2)}, u32[]{:S(2)}) collective-permute-start(bf16[160,960]{1,0:T(8,128)(2,1)S(1)} %collective-permute-done.6), channel_id=1, source_target_pairs={{8,0},{16,8},{24,16},{28,24},{20,28},{12,20},{4,12},{0,4},{9,1},{1... | collective-permute-start | bytes 921608 | tf_op jit(solution)/shard_map/ppermute | solution.py:60
  85.8 45.9 %collective-permute-start.2 = (bf16[256,1280]{1,0:T(8,128)(2,1)}, bf16[256,1280]{1,0:T(8,128)(2,1)}, u32[]{:S(2)}, u32[]{:S(2)}) collective-permute-start(bf16[256,1280]{1,0:T(8,128)(2,1)} %collective-permute-done.1), channel_id=1, source_target_pairs={{0,1},{1,0},{2,3},{3,2},{4,5},{5,4},{6,7},{7,6},{8,9},{9,8},{10,11... | collective-permute-start | bytes 1966088 | tf_op jit(solution)/shard_map/ppermute | solution.py:105
  93.6 37.4 %collective-permute-start.36 = (bf16[160,1280]{1,0:T(8,128)(2,1)S(1)}, bf16[160,1280]{1,0:T(8,128)(2,1)}, u32[]{:S(2)}, u32[]{:S(2)}) collective-permute-start(bf16[160,1280]{1,0:T(8,128)(2,1)S(1)} %collective-permute-done.34), channel_id=1, source_target_pairs={{8,0},{16,8},{24,16},{28,24},{20,28},{12,20},{4,12},{0,4},{9,1},{1... | collective-permute-start | bytes 1228808 | tf_op jit(solution)/shard_map/ppermute | solution.py:60
  123.9 62.4 %collective-permute-start.27 = (bf16[160,2560]{1,0:T(8,128)(2,1)}, bf16[160,2560]{1,0:T(8,128)(2,1)}, u32[]{:S(2)}, u32[]{:S(2)}) collective-permute-start(bf16[160,2560]{1,0:T(8,128)(2,1)} %collective-permute-done.25), channel_id=1, source_target_pairs={{0,8},{8,16},{16,24},{24,28},{28,20},{20,12},{12,4},{4,0},{1,9},{9... | collective-permute-start | bytes 2457608 | tf_op jit(solution)/shard_map/ppermute | solution.py:59
  128.9 46.1 %collective-permute-start.37 = (bf16[160,1280]{1,0:T(8,128)(2,1)}, bf16[160,1280]{1,0:T(8,128)(2,1)}, u32[]{:S(2)}, u32[]{:S(2)}) collective-permute-start(bf16[160,1280]{1,0:T(8,128)(2,1)} %collective-permute-done.35), channel_id=1, source_target_pairs={{0,8},{8,16},{16,24},{24,28},{28,20},{20,12},{12,4},{4,0},{1,9},{9... | collective-permute-start | bytes 1228808 | tf_op jit(solution)/shard_map/ppermute | solution.py:59
  130.5 57.7 %collective-permute-start.28 = (bf16[160,2560]{1,0:T(8,128)(2,1)}, bf16[160,2560]{1,0:T(8,128)(2,1)}, u32[]{:S(2)}, u32[]{:S(2)}) collective-permute-start(bf16[160,2560]{1,0:T(8,128)(2,1)} %collective-permute-done.26), channel_id=1, source_target_pairs={{8,0},{16,8},{24,16},{28,24},{20,28},{12,20},{4,12},{0,4},{9,1},{1... | collective-permute-start | bytes 2457608 | tf_op jit(solution)/shard_map/ppermute | solution.py:60
  131.0 46.6 %collective-permute-start.38 = (bf16[160,1280]{1,0:T(8,128)(2,1)}, bf16[160,1280]{1,0:T(8,128)(2,1)S(1)}, u32[]{:S(2)}, u32[]{:S(2)}) collective-permute-start(bf16[160,1280]{1,0:T(8,128)(2,1)} %collective-permute-done.36), channel_id=1, source_target_pairs={{8,0},{16,8},{24,16},{28,24},{20,28},{12,20},{4,12},{0,4},{9,1},{1... | collective-permute-start | bytes 1228808 | tf_op jit(solution)/shard_map/ppermute | solution.py:60
  183.5 16.3 %collective-permute-start.21 = (bf16[256,1280]{1,0:T(8,128)(2,1)S(1)}, bf16[256,1280]{1,0:T(8,128)(2,1)S(1)}, u32[]{:S(2)}, u32[]{:S(2)}) collective-permute-start(bf16[256,1280]{1,0:T(8,128)(2,1)S(1)} %fusion.75), channel_id=1, source_target_pairs={{0,2},{1,3},{2,0},{3,1},{4,6},{5,7},{6,4},{7,5},{8,10},{9,11},{10,... | collective-permute-start | bytes 1966088 | tf_op jit(solution)/shard_map/ppermute | solution.py:105
  186.3 20.2 %collective-permute-start.29 = (bf16[160,2560]{1,0:T(8,128)(2,1)}, bf16[160,2560]{1,0:T(8,128)(2,1)S(1)}, u32[]{:S(2)}, u32[]{:S(2)}) collective-permute-start(bf16[160,2560]{1,0:T(8,128)(2,1)} %collective-permute-done.27), channel_id=1, source_target_pairs={{0,8},{8,16},{16,24},{24,28},{28,20},{20,12},{12,4},{4,0},{1,9},{9... | collective-permute-start | bytes 2457608 | tf_op jit(solution)/shard_map/ppermute | solution.py:59
  188.2 19.9 %collective-permute-start.30 = (bf16[160,2560]{1,0:T(8,128)(2,1)}, bf16[160,2560]{1,0:T(8,128)(2,1)S(1)}, u32[]{:S(2)}, u32[]{:S(2)}) collective-permute-start(bf16[160,2560]{1,0:T(8,128)(2,1)} %collective-permute-done.28), channel_id=1, source_target_pairs={{8,0},{16,8},{24,16},{28,24},{20,28},{12,20},{4,12},{0,4},{9,1},{1... | collective-permute-start | bytes 2457608 | tf_op jit(solution)/shard_map/ppermute | solution.py:60
  201.3 15.5 %collective-permute-start.23 = (bf16[256,1280]{1,0:T(8,128)(2,1)S(1)}, bf16[256,1280]{1,0:T(8,128)(2,1)S(1)}, u32[]{:S(2)}, u32[]{:S(2)}) collective-permute-start(bf16[256,1280]{1,0:T(8,128)(2,1)S(1)} %multiply_convert_fusion.8), channel_id=1, source_target_pairs={{0,2},{1,3},{2,0},{3,1},{4,6},{5,7},{6,4},{7,5},{8,10},{9,11},{10,... | collective-permute-start | bytes 1966088 | tf_op jit(solution)/shard_map/ppermute | solution.py:105
  240.9 17.6 %collective-permute-start.41 = (bf16[256,1280]{1,0:T(8,128)(2,1)}, bf16[256,1280]{1,0:T(8,128)(2,1)}, u32[]{:S(2)}, u32[]{:S(2)}) collective-permute-start(bf16[256,1280]{1,0:T(8,128)(2,1)} %get-tuple-element.443), channel_id=1, source_target_pairs={{0,1},{1,0},{2,3},{3,2},{4,5},{5,4},{6,7},{7,6},{8,9},{9,8},{10,11... | collective-permute-start | bytes 1966088 | tf_op jit(solution)/shard_map/ppermute | solution.py:105
  244.0 17.3 %collective-permute-start.43 = (bf16[256,1280]{1,0:T(8,128)(2,1)}, bf16[256,1280]{1,0:T(8,128)(2,1)}, u32[]{:S(2)}, u32[]{:S(2)}) collective-permute-start(bf16[256,1280]{1,0:T(8,128)(2,1)} %fusion.73), channel_id=1, source_target_pairs={{0,2},{1,3},{2,0},{3,1},{4,6},{5,7},{6,4},{7,5},{8,10},{9,11},{10,... | collective-permute-start | bytes 1966088 | tf_op jit(solution)/shard_map/ppermute | solution.py:105
  268.9 16.5 %collective-permute-start.48 = (bf16[256,1280]{1,0:T(8,128)(2,1)}, bf16[256,1280]{1,0:T(8,128)(2,1)}, u32[]{:S(2)}, u32[]{:S(2)}) collective-permute-start(bf16[256,1280]{1,0:T(8,128)(2,1)} %multiply_convert_fusion.5), channel_id=1, source_target_pairs={{0,2},{1,3},{2,0},{3,1},{4,6},{5,7},{6,4},{7,5},{8,10},{9,11},{10,... | collective-permute-start | bytes 1966088 | tf_op jit(solution)/shard_map/ppermute | solution.py:105
  269.2 20.6 %collective-permute-start.47 = (bf16[256,1280]{1,0:T(8,128)(2,1)}, bf16[256,1280]{1,0:T(8,128)(2,1)}, u32[]{:S(2)}, u32[]{:S(2)}) collective-permute-start(bf16[256,1280]{1,0:T(8,128)(2,1)} %multiply_convert_fusion.5), channel_id=1, source_target_pairs={{0,1},{1,0},{2,3},{3,2},{4,5},{5,4},{6,7},{7,6},{8,9},{9,8},{10,11... | collective-permute-start | bytes 1966088 | tf_op jit(solution)/shard_map/ppermute | solution.py:105
  297.3 41.3 %collective-permute-start.80 = (bf16[160,640]{1,0:T(8,128)(2,1)}, bf16[160,640]{1,0:T(8,128)(2,1)}, u32[]{:S(2)}, u32[]{:S(2)}) collective-permute-start(bf16[160,640]{1,0:T(8,128)(2,1)} %get-tuple-element.435), channel_id=1, source_target_pairs={{0,8},{8,16},{16,24},{24,28},{28,20},{20,12},{12,4},{4,0},{1,9},{9... | collective-permute-start | bytes 614408 | tf_op jit(solution)/shard_map/ppermute | solution.py:85
  298.5 40.5 %collective-permute-start.84 = (bf16[160,640]{1,0:T(8,128)(2,1)}, bf16[160,640]{1,0:T(8,128)(2,1)}, u32[]{:S(2)}, u32[]{:S(2)}) collective-permute-start(bf16[160,640]{1,0:T(8,128)(2,1)} %get-tuple-element.437), channel_id=1, source_target_pairs={{8,0},{16,8},{24,16},{28,24},{20,28},{12,20},{4,12},{0,4},{9,1},{1... | collective-permute-start | bytes 614408 | tf_op jit(solution)/shard_map/ppermute | solution.py:86
  336.3 12.7 %collective-permute-start.76 = (bf16[160,1280]{1,0:T(8,128)(2,1)}, bf16[160,1280]{1,0:T(8,128)(2,1)}, u32[]{:S(2)}, u32[]{:S(2)}) collective-permute-start(bf16[160,1280]{1,0:T(8,128)(2,1)} %get-tuple-element.420), channel_id=1, source_target_pairs={{8,0},{16,8},{24,16},{28,24},{20,28},{12,20},{4,12},{0,4},{9,1},{1... | collective-permute-start | bytes 1228808 | tf_op jit(solution)/shard_map/ppermute | solution.py:86
  338.3 20.3 %collective-permute-start.51 = (bf16[256,1280]{1,0:T(8,128)(2,1)}, bf16[256,1280]{1,0:T(8,128)(2,1)}, u32[]{:S(2)}, u32[]{:S(2)}) collective-permute-start(bf16[256,1280]{1,0:T(8,128)(2,1)} %get-tuple-element.442), channel_id=1, source_target_pairs={{0,1},{1,0},{2,3},{3,2},{4,5},{5,4},{6,7},{7,6},{8,9},{9,8},{10,11... | collective-permute-start | bytes 1966088 | tf_op jit(solution)/shard_map/ppermute | solution.py:105
  338.6 49.3 %collective-permute-start.50 = (bf16[256,1280]{1,0:T(8,128)(2,1)}, bf16[256,1280]{1,0:T(8,128)(2,1)S(1)}, u32[]{:S(2)}, u32[]{:S(2)}) collective-permute-start(bf16[256,1280]{1,0:T(8,128)(2,1)} %get-tuple-element.441), channel_id=1, source_target_pairs={{0,1},{1,0},{2,3},{3,2},{4,5},{5,4},{6,7},{7,6},{8,9},{9,8},{10,11... | collective-permute-start | bytes 1966088 | tf_op jit(solution)/shard_map/ppermute | solution.py:105
  341.8 19.7 %collective-permute-start.85 = (bf16[160,1280]{1,0:T(8,128)(2,1)S(1)}, bf16[160,1280]{1,0:T(8,128)(2,1)S(1)}, u32[]{:S(2)}, u32[]{:S(2)}) collective-permute-start(bf16[160,1280]{1,0:T(8,128)(2,1)S(1)} %pad_maximum_fusion.23), channel_id=1, source_target_pairs={{8,0},{16,8},{24,16},{28,24},{20,28},{12,20},{4,12},{0,4},{9,1},{1... | collective-permute-start | bytes 1228808 | tf_op jit(solution)/shard_map/ppermute | solution.py:99
  350.7 58.0 %collective-permute-start.77 = (bf16[160,2560]{1,0:T(8,128)(2,1)S(1)}, bf16[160,2560]{1,0:T(8,128)(2,1)S(1)}, u32[]{:S(2)}, u32[]{:S(2)}) collective-permute-start(bf16[160,2560]{1,0:T(8,128)(2,1)S(1)} %pad_maximum_fusion.9), channel_id=1, source_target_pairs={{8,0},{16,8},{24,16},{28,24},{20,28},{12,20},{4,12},{0,4},{9,1},{1... | collective-permute-start | bytes 2457608 | tf_op jit(solution)/shard_map/ppermute | solution.py:99
  357.2 29.0 %collective-permute-start.73 = (bf16[160,2560]{1,0:T(8,128)(2,1)S(1)}, bf16[160,2560]{1,0:T(8,128)(2,1)S(1)}, u32[]{:S(2)}, u32[]{:S(2)}) collective-permute-start(bf16[160,2560]{1,0:T(8,128)(2,1)S(1)} %pad_maximum_fusion.8), channel_id=1, source_target_pairs={{0,8},{8,16},{16,24},{24,28},{28,20},{20,12},{12,4},{4,0},{1,9},{9... | collective-permute-start | bytes 2457608 | tf_op jit(solution)/shard_map/ppermute | solution.py:98
  358.6 25.7 %collective-permute-start.82 = (bf16[160,1280]{1,0:T(8,128)(2,1)S(1)}, bf16[160,1280]{1,0:T(8,128)(2,1)S(1)}, u32[]{:S(2)}, u32[]{:S(2)}) collective-permute-start(bf16[160,1280]{1,0:T(8,128)(2,1)S(1)} %add_convert_fusion.7), channel_id=1, source_target_pairs={{0,8},{8,16},{16,24},{24,28},{28,20},{20,12},{12,4},{4,0},{1,9},{9... | collective-permute-start | bytes 1228808 | tf_op jit(solution)/shard_map/ppermute | solution.py:98
  361.5 28.2 %collective-permute-start.52 = (bf16[256,1280]{1,0:T(8,128)(2,1)S(1)}, bf16[256,1280]{1,0:T(8,128)(2,1)S(1)}, u32[]{:S(2)}, u32[]{:S(2)}) collective-permute-start(bf16[256,1280]{1,0:T(8,128)(2,1)S(1)} %fusion.70), channel_id=1, source_target_pairs={{0,2},{1,3},{2,0},{3,1},{4,6},{5,7},{6,4},{7,5},{8,10},{9,11},{10,... | collective-permute-start | bytes 1966088 | tf_op jit(solution)/shard_map/ppermute | solution.py:105
  387.9 24.4 %collective-permute-start.74 = (bf16[160,2560]{1,0:T(8,128)(2,1)S(1)}, bf16[160,2560]{1,0:T(8,128)(2,1)S(1)}, u32[]{:S(2)}, u32[]{:S(2)}) collective-permute-start(bf16[160,2560]{1,0:T(8,128)(2,1)S(1)} %add_convert_fusion.3), channel_id=1, source_target_pairs={{0,8},{8,16},{16,24},{24,28},{28,20},{20,12},{12,4},{4,0},{1,9},{9... | collective-permute-start | bytes 2457608 | tf_op jit(solution)/shard_map/ppermute | solution.py:98
  396.1 12.5 %collective-permute-start.54 = (bf16[256,1280]{1,0:T(8,128)(2,1)S(1)}, bf16[256,1280]{1,0:T(8,128)(2,1)S(1)}, u32[]{:S(2)}, u32[]{:S(2)}) collective-permute-start(bf16[256,1280]{1,0:T(8,128)(2,1)S(1)} %multiply_convert_fusion.4), channel_id=1, source_target_pairs={{0,2},{1,3},{2,0},{3,1},{4,6},{5,7},{6,4},{7,5},{8,10},{9,11},{10,... | collective-permute-start | bytes 1966088 | tf_op jit(solution)/shard_map/ppermute | solution.py:105
  398.5 18.8 %collective-permute-start.53 = (bf16[256,1280]{1,0:T(8,128)(2,1)S(1)}, bf16[256,1280]{1,0:T(8,128)(2,1)S(1)}, u32[]{:S(2)}, u32[]{:S(2)}) collective-permute-start(bf16[256,1280]{1,0:T(8,128)(2,1)S(1)} %multiply_convert_fusion.4), channel_id=1, source_target_pairs={{0,1},{1,0},{2,3},{3,2},{4,5},{5,4},{6,7},{7,6},{8,9},{9,8},{10,11... | collective-permute-start | bytes 1966088 | tf_op jit(solution)/shard_map/ppermute | solution.py:105
  415.3 104.4 %collective-permute-start.78 = (bf16[160,2560]{1,0:T(8,128)(2,1)}, bf16[160,2560]{1,0:T(8,128)(2,1)}, u32[]{:S(2)}, u32[]{:S(2)}) collective-permute-start(bf16[160,2560]{1,0:T(8,128)(2,1)} %get-tuple-element.415), channel_id=1, source_target_pairs={{8,0},{16,8},{24,16},{28,24},{20,28},{12,20},{4,12},{0,4},{9,1},{1... | collective-permute-start | bytes 2457608 | tf_op jit(solution)/shard_map/ppermute | solution.py:99
  416.9 144.7 %collective-permute-start.75 = (bf16[160,2560]{1,0:T(8,128)(2,1)}, bf16[160,2560]{1,0:T(8,128)(2,1)}, u32[]{:S(2)}, u32[]{:S(2)}) collective-permute-start(bf16[160,2560]{1,0:T(8,128)(2,1)} %get-tuple-element.414), channel_id=1, source_target_pairs={{0,8},{8,16},{16,24},{24,28},{28,20},{20,12},{12,4},{4,0},{1,9},{9... | collective-permute-start | bytes 2457608 | tf_op jit(solution)/shard_map/ppermute | solution.py:98
  488.6 15.5 %collective-permute-start.56 = (f32[14081]{0:T(1024)S(1)}, f32[14081]{0:T(1024)S(1)}, u32[]{:S(2)}, u32[]{:S(2)}) collective-permute-start(f32[14081]{0:T(1024)S(1)} %concatenate.58), channel_id=1, source_target_pairs={{0,1},{1,0},{2,3},{3,2},{4,5},{5,4},{6,7},{7,6},{8,9},{9,8},{10,11... | collective-permute-start | bytes 168980 | tf_op jit(solution)/shard_map/ppermute | solution.py:105
  514.5 27.0 %collective-permute-start.62 = (bf16[256,1280]{1,0:T(8,128)(2,1)S(1)}, bf16[256,1280]{1,0:T(8,128)(2,1)S(1)}, u32[]{:S(2)}, u32[]{:S(2)}) collective-permute-start(bf16[256,1280]{1,0:T(8,128)(2,1)S(1)} %get-tuple-element.440), channel_id=1, source_target_pairs={{0,1},{1,0},{2,3},{3,2},{4,5},{5,4},{6,7},{7,6},{8,9},{9,8},{10,11... | collective-permute-start | bytes 1966088 | tf_op jit(solution)/shard_map/ppermute | solution.py:105
  514.5 52.0 %collective-permute-start.61 = (bf16[256,1280]{1,0:T(8,128)(2,1)S(1)}, bf16[256,1280]{1,0:T(8,128)(2,1)S(1)}, u32[]{:S(2)}, u32[]{:S(2)}) collective-permute-start(bf16[256,1280]{1,0:T(8,128)(2,1)S(1)} %get-tuple-element.439), channel_id=1, source_target_pairs={{0,1},{1,0},{2,3},{3,2},{4,5},{5,4},{6,7},{7,6},{8,9},{9,8},{10,11... | collective-permute-start | bytes 1966088 | tf_op jit(solution)/shard_map/ppermute | solution.py:105
  519.4 15.0 %collective-permute-start.69 = (bf16[160,1280]{1,0:T(8,128)(2,1)S(1)}, bf16[160,1280]{1,0:T(8,128)(2,1)S(1)}, u32[]{:S(2)}, u32[]{:S(2)}) collective-permute-start(bf16[160,1280]{1,0:T(8,128)(2,1)S(1)} %pad_maximum_fusion.21), channel_id=1, source_target_pairs={{8,0},{16,8},{24,16},{28,24},{20,28},{12,20},{4,12},{0,4},{9,1},{1... | collective-permute-start | bytes 1228808 | tf_op jit(solution)/shard_map/ppermute | solution.py:99
  534.4 29.1 %collective-permute-start.79 = (bf16[160,2560]{1,0:T(8,128)(2,1)S(1)}, bf16[160,2560]{1,0:T(8,128)(2,1)S(1)}, u32[]{:S(2)}, u32[]{:S(2)}) collective-permute-start(bf16[160,2560]{1,0:T(8,128)(2,1)S(1)} %add_convert_fusion), channel_id=1, source_target_pairs={{8,0},{16,8},{24,16},{28,24},{20,28},{12,20},{4,12},{0,4},{9,1},{1... | collective-permute-start | bytes 2457608 | tf_op jit(solution)/shard_map/ppermute | solution.py:99
  541.5 19.7 %collective-permute-start.70 = (bf16[160,1280]{1,0:T(8,128)(2,1)S(1)}, bf16[160,1280]{1,0:T(8,128)(2,1)S(1)}, u32[]{:S(2)}, u32[]{:S(2)}) collective-permute-start(bf16[160,1280]{1,0:T(8,128)(2,1)S(1)} %get-tuple-element.427), channel_id=1, source_target_pairs={{8,0},{16,8},{24,16},{28,24},{20,28},{12,20},{4,12},{0,4},{9,1},{1... | collective-permute-start | bytes 1228808 | tf_op jit(solution)/shard_map/ppermute | solution.py:99
  549.4 17.1 %collective-permute-start.63 = (bf16[256,1280]{1,0:T(8,128)(2,1)S(1)}, bf16[256,1280]{1,0:T(8,128)(2,1)S(1)}, u32[]{:S(2)}, u32[]{:S(2)}) collective-permute-start(bf16[256,1280]{1,0:T(8,128)(2,1)S(1)} %fusion.66), channel_id=1, source_target_pairs={{0,2},{1,3},{2,0},{3,1},{4,6},{5,7},{6,4},{7,5},{8,10},{9,11},{10,... | collective-permute-start | bytes 1966088 | tf_op jit(solution)/shard_map/ppermute | solution.py:105
  (130 other events, 1334.3 us)
